TPU v7x, 32 devices: a whole 2x2x4 slice. The times are simulated.
32 devices in a mesh: seq: 16 (over z, y, x), head: 2 (over core).
Axes of the slice: x: 2, y: 2, z: 4, core: 2. Of those that a mesh axis runs over, the one named last changes fastest.
Arguments:
- queries: bfloat16 [4096, 4096], P('seq', 'head'), may hold values from -12 to 12
- key_input: bfloat16 [4096, 4096], P('seq', 'head'), may hold values from -1.796875 to 1.796875
- value_input: bfloat16 [4096, 4096], P('seq', 'head'), may hold values from -32 to 32
- norm_gain: bfloat16 [4096], P('head'), may hold values from 0.099609375 to 1.8984375
- out_weight: bfloat16 [4096, 3072], P('head', 'seq'), may hold values from -0.125 to 0.125
- target: bfloat16 [4096, 3072], P('seq', 'head'), may hold values from -6 to 6
Outputs:
- output: bfloat16 [4096, 3072], P('seq', 'head')
- query_grad: bfloat16 [4096, 4096], P('seq', 'head')
- key_grad: bfloat16 [4096, 4096], P('seq', 'head')
- value_grad: bfloat16 [4096, 4096], P('seq', 'head')
- gain_grads: float32 [16, 4096], P('seq', 'head')
- weight_grads: bfloat16 [16, 4096, 3072], P('seq', 'head')
All inputs are finite; a program needn't handle non-finite values.
Results may differ from a plain program's by a relative error of at most 0.022.
Values may be sent and summed in bfloat16 or wider, within the bound.
A program may use at most 128 MiB of HBM per device.

v0:
```python
import jax
import jax.numpy as jnp
from jax import lax
from jax.sharding import PartitionSpec as P

HEAD_DIM = 128
FEATURES = 4096


EPSILON = 1e-06


def entering(shard, axis, join, neutral, backward):
    count = lax.axis_size(axis)
    place = lax.axis_index(axis)
    ahead = count - 1 - place if backward else place
    gathered = lax.all_gather(shard.astype(jnp.bfloat16), axis)
    state = jnp.zeros_like(shard) + jnp.asarray(neutral, shard.dtype)

    def one(step, state):
        source = count - 1 - step if backward else step
        return join(state, lax.dynamic_index_in_dim(gathered, source, 0, False).astype(shard.dtype))

    return lax.fori_loop(0, ahead, one, state)


def causal(count):
    row_index = lax.broadcasted_iota(jnp.int32, (count, count), 0)
    col_index = lax.broadcasted_iota(jnp.int32, (count, count), 1)
    return row_index >= col_index


def add_states(earlier, later):
    return earlier + later


def per_device(queries, key_input, value_input, norm_gain, out_weight, target):
    tok_count = queries.shape[0]
    local_heads = queries.shape[1] // HEAD_DIM
    shape3 = (tok_count, local_heads, HEAD_DIM)
    q_heads = queries.reshape(shape3)
    k_heads = key_input.reshape(shape3)
    v_heads = value_input.reshape(shape3)
    keep_mask = causal(tok_count)
    f32 = jnp.float32
    state_local = jnp.einsum("shd,she->hde", k_heads, v_heads, preferred_element_type=f32)
    zero_state = jnp.zeros_like(state_local)
    earlier_state = entering(state_local, "seq", add_states, zero_state, False)
    state_low = earlier_state.astype(jnp.bfloat16)
    scores = jnp.einsum("thd,shd->hts", q_heads, k_heads, preferred_element_type=f32)
    scores_low = jnp.where(keep_mask[None], scores, 0.0).astype(jnp.bfloat16)
    attended = jnp.einsum("hts,shd->thd", scores_low, v_heads, preferred_element_type=f32)
    attended = attended + jnp.einsum("thd,hde->the", q_heads, state_low, preferred_element_type=f32)
    mixed = attended.reshape(tok_count, -1)
    gain_float = norm_gain.astype(f32)
    squares = lax.psum(jnp.sum(mixed * mixed, axis=1, keepdims=True), "head")
    inverse = lax.rsqrt(squares / FEATURES + EPSILON)
    normed = (mixed * inverse * gain_float).astype(jnp.bfloat16)
    full_weight = lax.all_gather(out_weight, "seq", axis=1, tiled=True)
    partial_value = jnp.dot(normed, full_weight, preferred_element_type=f32)
    projected = lax.psum_scatter(
        partial_value.astype(jnp.bfloat16), "head", scatter_dimension=1, tiled=True
    ).astype(jnp.float32)
    output = projected.astype(jnp.bfloat16)
    grad_local = (projected - target.astype(f32)).astype(jnp.bfloat16)
    out_grad = lax.all_gather(grad_local, "head", axis=1, tiled=True)
    normed_grad = lax.dot_general(
        out_grad, full_weight, (((1,), (1,)), ((), ())), preferred_element_type=f32
    )
    product = jnp.sum(grad_local.astype(f32) * projected, axis=1, keepdims=True)
    inner = lax.psum(product, "head") / inverse
    mixed_grad = inverse * gain_float * normed_grad - mixed * inverse**3 * inner / FEATURES
    mixed_grad = mixed_grad.astype(jnp.bfloat16)
    gain_grads = jnp.sum(normed_grad * mixed * inverse, axis=0)[None]
    weight_grads = lax.dot_general(
        normed, out_grad, (((0,), (0,)), ((), ())), preferred_element_type=f32
    ).astype(jnp.bfloat16)[None]
    grad_heads = mixed_grad.reshape(shape3)
    grad_state = jnp.einsum("thd,the->hde", q_heads, grad_heads, preferred_element_type=f32)
    later_state = entering(grad_state, "seq", add_states, zero_state, True)
    later_low = later_state.astype(jnp.bfloat16)
    pairs = jnp.einsum("thd,shd->hts", grad_heads, v_heads, preferred_element_type=f32)
    pairs_low = jnp.where(keep_mask[None], pairs, 0.0).astype(jnp.bfloat16)
    query_grad = jnp.einsum("hts,shd->thd", pairs_low, k_heads, preferred_element_type=f32)
    query_grad = query_grad + jnp.einsum(
        "the,hde->thd", grad_heads, state_low, preferred_element_type=f32
    )
    key_grad = jnp.einsum("hts,thd->shd", pairs_low, q_heads, preferred_element_type=f32)
    key_grad = key_grad + jnp.einsum("she,hde->shd", v_heads, later_low, preferred_element_type=f32)
    value_grad = jnp.einsum("hts,the->she", scores_low, grad_heads, preferred_element_type=f32)
    value_grad = value_grad + jnp.einsum(
        "shd,hde->she", k_heads, later_low, preferred_element_type=f32
    )
    flat_shape = (tok_count, -1)
    return (
        output,
        query_grad.reshape(flat_shape).astype(jnp.bfloat16),
        key_grad.reshape(flat_shape).astype(jnp.bfloat16),
        value_grad.reshape(flat_shape).astype(jnp.bfloat16),
        gain_grads,
        weight_grads,
    )


def solution(mesh):
    placed = (
        P("seq", "head"),
        P("seq", "head"),
        P("seq", "head"),
        P("head"),
        P("head", "seq"),
        P("seq", "head"),
    )
    return jax.shard_map(
        per_device,
        mesh=mesh,
        in_specs=placed,
        out_specs=(
            P("seq", "head"),
            P("seq", "head"),
            P("seq", "head"),
            P("seq", "head"),
            P("seq", "head"),
            P("seq", "head", None),
        ),
        check_vma=False,
    )
```

profile of v0, /device:TPU:0, one launch (start us, length us, event | category | flops | bytes accessed | tf_op | source)
XLA Modules:
  0.0 477.5 jit_solution(6692178942128432424)
XLA Ops:
  7.2 2.6 copy.93
  16.9 2.2 fusion.5
  19.1 108.8 %all-gather.11.cloned.1.call-done = bf16[256,128,128]{2,1,0:T(8,128)(2,1)} async-done(((bf16[16,128,128]{2,1,0:T(8,128)(2,1)}), bf16[256,128,128]{2,1,0:T(8,128)(2,1)}) %all-gather.11.cloned.1.call-update) | async-done | bytes 8388624 | tf_op jit(solution)/shard_map/all_gather | solution.py:17
  128.0 3.4 multiply_reduce_fusion.1
  131.4 2.9 copy.69
  134.3 2.4 psum.14
  136.8 143.5 %all-gather.7.cloned.1.call-done = bf16[2048,3072]{0,1:T(8,128)(2,1)} async-done(((bf16[2048,192]{0,1:T(8,128)(2,1)}), bf16[2048,3072]{0,1:T(8,128)(2,1)}) %all-gather.7.cloned.1.call-update) | async-done | bytes 12582928 | tf_op jit(solution)/shard_map/all_gather | solution.py:59
  280.3 9.9 %convolution_convert_fusion = bf16[256,3072]{1,0:T(8,128)(2,1)} fusion(bf16[2048,3072]{0,1:T(8,128)(2,1)} %all-gather.7.cloned.1.call-done, f32[256,2048]{1,0:T(8,128)} %copy.69, f32[2048]{0:T(1024)S(1)} %convert_element_type.88, f32[256]{0:T(256)S(1)} %bitcast.131), kind=kOutput, calls=%fused_computation.5 | convolution fusion | flops 3223584768 | bytes 16262144 | tf_op jit(solution)/shard_map/dot_general | solution.py:60
  290.2 7.2 %reduce-scatter.2.cloned.1.call-done = bf16[256,1536]{1,0:T(8,128)(2,1)} async-done(((bf16[256,3072]{1,0:T(8,128)(2,1)}), bf16[256,1536]{1,0:T(8,128)(2,1)}) %reduce-scatter.2.cloned.1.call-update) | async-done | bytes 786448 | tf_op jit(solution)/shard_map/reduce_scatter | solution.py:61
  297.5 2.3 fusion.3
  299.8 2.7 psum.15
  302.5 8.5 %all-gather.9.cloned.1.call-done = bf16[256,3072]{1,0:T(8,128)(2,1)} async-done(((bf16[256,1536]{1,0:T(8,128)(2,1)}), bf16[256,3072]{1,0:T(8,128)(2,1)}) %all-gather.9.cloned.1.call-update) | async-done | bytes 1572880 | tf_op jit(solution)/shard_map/all_gather | solution.py:66
  311.0 11.0 %multiply_reduce_fusion = (f32[2048]{0:T(1024)}, bf16[256,2048]{1,0:T(8,128)(2,1)}) fusion(f32[256,2048]{1,0:T(8,128)} %copy.69, f32[256]{0:T(256)S(1)} %bitcast.132, f32[256]{0:T(256)S(1)} %bitcast.137, f32[256]{0:T(256)S(1)} %bitcast.136, f32[2048]{0:T(1024)S(1)} %convert_element_type.88, bf16[256,3072]{1,0:T(8,128)(2,1)} %all-gather.9.cloned.1.call-done, ...), kind=kOutput, calls=%fused_computation.11 | convolution fusion | flops 3226466304 | bytes 17320960 | tf_op jit(solution)/shard_map/dot_general | solution.py:67
  324.7 2.1 copy.78
  326.8 2.1 select_convert_fusion
  331.7 2.3 copy.84
  333.9 3.5 fusion.32
  340.3 6.7 %convert_bitcast_fusion = bf16[1,2048,3072]{2,1,0:T(8,128)(2,1)} fusion(bf16[256,3072]{1,0:T(8,128)(2,1)S(1)} %copy-done.10, f32[256,2048]{1,0:T(8,128)S(1)} %copy-done.1, f32[2048]{0:T(1024)S(1)} %convert_element_type.88, f32[256]{0:T(256)S(1)} %bitcast.133), kind=kOutput, calls=%fused_computation.2 | convolution fusion | flops 3229089792 | bytes 16262144 | tf_op jit(solution)/shard_map/dot_general | solution.py:75
  347.0 93.4 %all-gather.13.cloned.1.call-done = bf16[256,128,128]{2,1,0:T(8,128)(2,1)} async-done(((bf16[16,128,128]{2,1,0:T(8,128)(2,1)}), bf16[256,128,128]{2,1,0:T(8,128)(2,1)}) %all-gather.13.cloned.1.call-update) | async-done | bytes 8388624 | tf_op jit(solution)/shard_map/all_gather | solution.py:17
  440.5 19.7 %while.23 = (s32[]{:T(128)}, f32[16,128,128]{2,1,0:T(8,128)S(1)}, s32[]{:T(128)}, bf16[16,16,128,128]{3,2,1,0:T(8,128)(2,1)}, s32[]{:T(128)}, /*index=5*/s32[]{:T(128)}, s32[]{:T(128)}, s32[]{:T(128)}) while((s32[]{:T(128)}, f32[16,128,128]{2,1,0:T(8,128)S(1)}, s32[]{:T(128)}, bf16[16,16,128,128]{3,2,1,0:T(8,128)(2,1)}, s32[]{:T(128)}, ...), condition=%wide.region_8.9_spmd, body=%wide.region_7.8_spmd.sunk | while | flops 524294 | bytes 2621575 | solution.py:24
  460.3 3.1 add_convert_fusion
  463.3 2.4 copy.86
  465.7 3.0 fusion
  468.7 2.3 copy.85
  (66 shorter events, 35.0 us)
Async XLA Ops:
  7.2 6.4 %copy-start = (bf16[256,2048]{1,0:T(8,128)(2,1)S(1)}, bf16[256,2048]{1,0:T(8,128)(2,1)}, u32[]{:S(2)}) copy-start(bf16[256,2048]{1,0:T(8,128)(2,1)} %param.10) | copy-start | bytes 3145732
  7.2 120.7 %all-gather.11.cloned.1.call-start = ((), (), s32[]{:S(2)}) async-start(), calls=%async_computation.4 | async-start | bytes 8912896 | tf_op jit(solution)/shard_map/all_gather | solution.py:17
  7.2 4.2 copy-start.2
  11.5 4.1 copy-start.4
  11.5 2.1 copy-start.12
  12.7 267.6 %all-gather.7.cloned.1.call-start = ((), (), s32[]{:S(2)}) async-start(), calls=%async_computation.1 | async-start | bytes 13369344 | tf_op jit(solution)/shard_map/all_gather | solution.py:59
  13.5 284.0 %reduce-scatter.2.cloned.1.call-start = ((), (), s32[]{:S(2)}) async-start(), calls=%async_computation.2 | async-start | bytes 2359296 | tf_op jit(solution)/shard_map/reduce_scatter | solution.py:61
  15.5 1.4 copy-start.6
  290.1 7.3 %copy-start.11 = (bf16[256,1536]{1,0:T(8,128)(2,1)S(1)}, bf16[256,1536]{1,0:T(8,128)(2,1)}, u32[]{:S(2)}) copy-start(bf16[256,1536]{1,0:T(8,128)(2,1)} %param.15) | copy-start | bytes 2359300
  290.2 20.8 %all-gather.9.cloned.1.call-start = ((), (), s32[]{:S(2)}) async-start(), calls=%async_computation.3 | async-start | bytes 2359296 | tf_op jit(solution)/shard_map/all_gather | solution.py:66
  299.8 140.6 %all-gather.13.cloned.1.call-start = ((), (), s32[]{:S(2)}) async-start(), calls=%async_computation.5 | async-start | bytes 8912896 | tf_op jit(solution)/shard_map/all_gather | solution.py:17
  326.8 2.1 copy-start.5
  328.9 1.3 copy-start.7
  333.9 3.5 copy-start.8
  337.5 2.0 copy-start.1
  337.5 2.9 copy-start.10
  440.5 19.8 %copy-start.9 = (bf16[256,2048]{1,0:T(8,128)(2,1)S(1)}, bf16[256,2048]{1,0:T(8,128)(2,1)}, u32[]{:S(2)}) copy-start(bf16[256,2048]{1,0:T(8,128)(2,1)} %param.11) | copy-start | bytes 3145732
  463.3 2.4 copy-start.3
Sparse Core Ops, SparseCore 0:
  12.8 115.0 all-gather.10
  130.7 149.5 all-gather.6
  290.3 7.1 reduce-scatter.1
  299.9 11.0 all-gather.8
  326.9 113.4 all-gather.12
where the time goes:
time: 479 us; the launch traced here: 478 us
  waiting for transfers between devices  362 us (76%)
  matrix products  53.3 us (11%)
  other arithmetic  21.7 us (5%)
  local copies, waits for them, and re-layouts  20.6 us (4%)
  between operations  14 us (3%)
  blocking collectives  5.09 us (1%)
    all_gather x2, waiting for transfers between devices, entering(): gathered = lax.all_gather(shard.astype(jnp.bfloat16), axis)  202 us
    all_gather x1, waiting for transfers between devices, per_device(): full_weight = lax.all_gather(out_weight, 'seq', axis=1, tiled=True)  143 us
    add x15, other arithmetic, add_states(): return earlier + later  19.3 us
    unnamed x30, local copies, waits for them, and re-layouts  12.3 us
    dot_general x1, matrix products, per_device(): lax.dot_general(out_grad, full_weight, (((1,), (1,)), ((), ())), preferre...  11 us
    dot_general x1, matrix products, per_device(): partial_value = jnp.dot(normed, full_weight, preferred_element_type=f32)  9.86 us
  transfers between devices with their start and end apart: 5, of which 5 were waited for; matrix products, arithmetic and copies ran while one was open for 6% of the time, Pallas kernels for 0%

commit v1 on v0

--- a/solution.py
+++ b/solution.py
@@ -10,28 +10,23 @@
 EPSILON = 1e-06
 
 
-def entering(shard, axis, join, neutral, backward):
+def entering(shard, axis, backward):
     count = lax.axis_size(axis)
-    place = lax.axis_index(axis)
-    ahead = count - 1 - place if backward else place
-    gathered = lax.all_gather(shard.astype(jnp.bfloat16), axis)
-    state = jnp.zeros_like(shard) + jnp.asarray(neutral, shard.dtype)
-
-    def one(step, state):
-        source = count - 1 - step if backward else step
-        return join(state, lax.dynamic_index_in_dim(gathered, source, 0, False).astype(shard.dtype))
-
-    return lax.fori_loop(0, ahead, one, state)
+    pieces = shard.astype(jnp.bfloat16).reshape(count, -1, shard.shape[-1])
+    spread = lax.all_to_all(pieces, axis, 0, 0)
+    row_index = lax.broadcasted_iota(jnp.int32, (count, count), 0)
+    col_index = lax.broadcasted_iota(jnp.int32, (count, count), 1)
+    chosen = col_index > row_index if backward else col_index < row_index
+    sums = jnp.einsum(
+        "ij,jrc->irc", chosen.astype(jnp.bfloat16), spread, preferred_element_type=jnp.float32
+    )
+    return lax.all_to_all(sums.astype(jnp.bfloat16), axis, 0, 0).reshape(shard.shape)
 
 
 def causal(count):
     row_index = lax.broadcasted_iota(jnp.int32, (count, count), 0)
     col_index = lax.broadcasted_iota(jnp.int32, (count, count), 1)
     return row_index >= col_index
-
-
-def add_states(earlier, later):
-    return earlier + later
 
 
 def per_device(queries, key_input, value_input, norm_gain, out_weight, target):
@@ -44,9 +39,7 @@
     keep_mask = causal(tok_count)
     f32 = jnp.float32
     state_local = jnp.einsum("shd,she->hde", k_heads, v_heads, preferred_element_type=f32)
-    zero_state = jnp.zeros_like(state_local)
-    earlier_state = entering(state_local, "seq", add_states, zero_state, False)
-    state_low = earlier_state.astype(jnp.bfloat16)
+    state_low = entering(state_local, "seq", False)
     scores = jnp.einsum("thd,shd->hts", q_heads, k_heads, preferred_element_type=f32)
     scores_low = jnp.where(keep_mask[None], scores, 0.0).astype(jnp.bfloat16)
     attended = jnp.einsum("hts,shd->thd", scores_low, v_heads, preferred_element_type=f32)
@@ -77,8 +70,7 @@
     ).astype(jnp.bfloat16)[None]
     grad_heads = mixed_grad.reshape(shape3)
     grad_state = jnp.einsum("thd,the->hde", q_heads, grad_heads, preferred_element_type=f32)
-    later_state = entering(grad_state, "seq", add_states, zero_state, True)
-    later_low = later_state.astype(jnp.bfloat16)
+    later_low = entering(grad_state, "seq", True)
     pairs = jnp.einsum("thd,shd->hts", grad_heads, v_heads, preferred_element_type=f32)
     pairs_low = jnp.where(keep_mask[None], pairs, 0.0).astype(jnp.bfloat16)
     query_grad = jnp.einsum("hts,shd->thd", pairs_low, k_heads, preferred_element_type=f32)

time: 479 us -> 289 us (0.60)
  waiting for transfers between devices: 362 us -> 140 us
  blocking collectives: 5.09 us -> 35.6 us
  starting transfers between devices: 0.2 us -> 19.7 us
  other arithmetic: 21.7 us -> 2.58 us
    all_gather x2 -> x0, waiting for transfers between devices: 202 us -> none  [entering(): gathered = lax.all_gather(shard.astype(jnp.bfloat16), axis)]
    all_gather x1, waiting for transfers between devices: 143 us -> 96.6 us  [per_device(): full_weight = lax.all_gather(out_weight, 'seq', axis=1, tiled=True)]
    all_to_all x0 -> x1, blocking collectives: none -> 30.5 us  [entering(): spread = lax.all_to_all(pieces, axis, 0, 0)]
    all_to_all x0 -> x3, waiting for transfers between devices: none -> 26.6 us  [the longest x2 18.8 us: entering(): lax.all_to_all(sums.astype(jnp.bfloat16), axis, 0, 0).reshape(shard.shape)]
    all_to_all x0 -> x3, starting transfers between devices: none -> 19.6 us  [the longest x2 12.7 us: entering(): lax.all_to_all(sums.astype(jnp.bfloat16), axis, 0, 0).reshape(shard.shape)]
    add x15 -> x0, other arithmetic: 19.3 us -> none  [add_states(): return earlier + later]
    unnamed x30 -> x34, local copies, waits for them, and re-layouts: 12.3 us -> 10 us
  transfers between devices with their start and end apart: 5 -> 6, of which waited for: 5 -> 6; matrix products, arithmetic and copies ran while one was open for 6% -> 11% of each run, Pallas kernels for 0% -> 0%
where the time goes in v1:
time: 289 us; the launch traced here: 288 us
  waiting for transfers between devices  140 us (48%)
  matrix products  57.7 us (20%)
  blocking collectives  35.6 us (12%)
  starting transfers between devices  19.7 us (7%)
  local copies, waits for them, and re-layouts  19.1 us (7%)
  between operations  14 us (5%)
    all_gather x1, waiting for transfers between devices, per_device(): full_weight = lax.all_gather(out_weight, 'seq', axis=1, tiled=True)  96.6 us
    all_to_all x1, blocking collectives, entering(): spread = lax.all_to_all(pieces, axis, 0, 0)  30.5 us
    all_to_all x2, waiting for transfers between devices, entering(): lax.all_to_all(sums.astype(jnp.bfloat16), axis, 0, 0).reshape(shard.shape)  18.8 us
    dot_general x1, matrix products, per_device(): partial_value = jnp.dot(normed, full_weight, preferred_element_type=f32)  14 us
    all_to_all x2, starting transfers between devices, entering(): lax.all_to_all(sums.astype(jnp.bfloat16), axis, 0, 0).reshape(shard.shape)  12.7 us
    dot_general x1, matrix products, per_device(): lax.dot_general(out_grad, full_weight, (((1,), (1,)), ((), ())), preferre...  10.4 us
    unnamed x34, local copies, waits for them, and re-layouts  10 us
    all_gather x1, waiting for transfers between devices, per_device(): out_grad = lax.all_gather(grad_local, 'head', axis=1, tiled=True)  8.6 us
  transfers between devices with their start and end apart: 6, of which 6 were waited for; matrix products, arithmetic and copies ran while one was open for 11% of the time, Pallas kernels for 0%

profile of v1, /device:TPU:0, one launch (start us, length us, event | category | flops | bytes accessed | tf_op | source)
XLA Modules:
  0.0 288.4 jit_solution(15459992873029129070)
XLA Ops:
  7.9 2.5 copy.91
  12.5 30.5 %all_to_all.20 = bf16[16,128,128]{2,1,0:T(8,128)(2,1)S(1)} all-to-all(bf16[16,128,128]{2,1,0:T(8,128)(2,1)S(1)} %convolution_convert_fusion.4), channel_id=1, replica_groups=mesh['seq'=16,'head'=2] {'seq'}, dimensions={0} | all-to-all | bytes 1048576 | tf_op jit(solution)/shard_map/all_to_all | solution.py:16
  44.4 8.5 %all-to-all-start.1 = ((bf16[16,128,128]{2,1,0:T(8,128)(2,1)}), bf16[16,128,128]{2,1,0:T(8,128)(2,1)S(1)}, u32[]{:S(2)}, u32[]{:S(2)}) async-start(bf16[16,128,128]{2,1,0:T(8,128)(2,1)} %copy.62), calls=%async_computation.1 | async-start | bytes 1048576 | tf_op jit(solution)/shard_map/all_to_all | solution.py:23
  56.3 2.2 fusion.5
  58.4 14.0 %all-to-all-done.1 = bf16[16,128,128]{2,1,0:T(8,128)(2,1)S(1)} async-done(((bf16[16,128,128]{2,1,0:T(8,128)(2,1)}), bf16[16,128,128]{2,1,0:T(8,128)(2,1)S(1)}, u32[]{:S(2)}, u32[]{:S(2)}) %all-to-all-start.1) | async-done | bytes 524320 | tf_op jit(solution)/shard_map/all_to_all | solution.py:23
  72.4 3.6 %multiply_reduce_fusion.1 = (f32[256]{0:T(256)S(1)}, f32[256,16,128]{0,2,1:T(8,128)}) fusion(bf16[16,128,128]{2,1,0:T(8,128)(2,1)S(1)} %all-to-all-done.1, f32[16,256,128]{1,2,0:T(8,128)} %fusion.5, bf16[256,2048]{1,0:T(8,128)(2,1)S(1)} %copy-done), kind=kOutput, calls=%fused_computation.13 | convolution fusion | flops 135790336 | bytes 5768192 | tf_op jit(solution)/shard_map/thd,hde->the/dot_general | solution.py:46
  78.0 2.5 psum.14
  80.5 96.6 %all-gather.3.cloned.1.call-done = bf16[2048,3072]{0,1:T(8,128)(2,1)} async-done(((bf16[2048,192]{0,1:T(8,128)(2,1)}), bf16[2048,3072]{0,1:T(8,128)(2,1)}) %all-gather.3.cloned.1.call-update) | async-done | bytes 12582928 | tf_op jit(solution)/shard_map/all_gather | solution.py:52
  177.0 14.0 %convolution_convert_fusion = bf16[256,3072]{1,0:T(8,128)(2,1)} fusion(bf16[2048,3072]{0,1:T(8,128)(2,1)} %all-gather.3.cloned.1.call-done, f32[256,2048]{1,0:T(8,128)S(1)} %copy.65, f32[2048]{0:T(1024)S(1)} %convert_element_type.75, f32[256]{0:T(256)S(1)} %bitcast.127), kind=kOutput, calls=%fused_computation.3 | convolution fusion | flops 3223584768 | bytes 16262144 | tf_op jit(solution)/shard_map/dot_general | solution.py:53
  191.1 7.2 %reduce-scatter.2.cloned.1.call-done = bf16[256,1536]{1,0:T(8,128)(2,1)} async-done(((bf16[256,3072]{1,0:T(8,128)(2,1)}), bf16[256,1536]{1,0:T(8,128)(2,1)}) %reduce-scatter.2.cloned.1.call-update) | async-done | bytes 786448 | tf_op jit(solution)/shard_map/reduce_scatter | solution.py:54
  198.4 2.5 fusion.3
  200.9 2.7 psum.15
  203.6 8.6 %all-gather.5.cloned.1.call-done = bf16[256,3072]{1,0:T(8,128)(2,1)} async-done(((bf16[256,1536]{1,0:T(8,128)(2,1)}), bf16[256,3072]{1,0:T(8,128)(2,1)}) %all-gather.5.cloned.1.call-update) | async-done | bytes 1572880 | tf_op jit(solution)/shard_map/all_gather | solution.py:59
  212.2 10.4 %multiply_reduce_fusion = (f32[2048]{0:T(1024)}, bf16[256,2048]{1,0:T(8,128)(2,1)}) fusion(f32[256,2048]{1,0:T(8,128)S(1)} %copy.65, f32[256]{0:T(256)S(1)} %bitcast.128, f32[256]{0:T(256)S(1)} %bitcast.133, f32[256]{0:T(256)S(1)} %bitcast.132, f32[2048]{0:T(1024)S(1)} %convert_element_type.75, bf16[256,3072]{1,0:T(8,128)(2,1)} %all-gather.5.cloned.1.call-done, ...), kind=kOutput, calls=%fused_computation.9 | convolution fusion | flops 3226466304 | bytes 17320960 | tf_op jit(solution)/shard_map/dot_general | solution.py:60
  229.7 6.8 %all-to-all-start.2 = ((bf16[16,128,128]{2,1,0:T(8,128)(2,1)}), bf16[16,128,128]{2,1,0:T(8,128)(2,1)}, u32[]{:S(2)}, u32[]{:S(2)}) async-start(bf16[16,128,128]{2,1,0:T(8,128)(2,1)} %copy.74), calls=%async_computation.3 | async-start | bytes 1048576 | tf_op jit(solution)/shard_map/all_to_all | solution.py:16
  236.5 2.5 fusion.33
  240.9 3.4 %fusion.34 = f32[16,128,256]{2,1,0:T(8,128)} fusion(bf16[256,16,128]{0,2,1:T(8,128)(2,1)S(1)} %bitcast.120, bf16[16,256,256]{2,1,0:T(8,128)(2,1)} %copy-done.8), kind=kOutput, calls=%fused_computation.55 | convolution fusion | flops 268435456 | bytes 5242880 | tf_op jit(solution)/shard_map/hts,the->she/dot_general | solution.py:82
  244.3 7.8 %all-to-all-done.2 = bf16[16,128,128]{2,1,0:T(8,128)(2,1)} async-done(((bf16[16,128,128]{2,1,0:T(8,128)(2,1)}), bf16[16,128,128]{2,1,0:T(8,128)(2,1)}, u32[]{:S(2)}, u32[]{:S(2)}) %all-to-all-start.2) | async-done | bytes 524320 | tf_op jit(solution)/shard_map/all_to_all | solution.py:16
  254.4 4.2 %all-to-all-start.3 = ((bf16[16,128,128]{2,1,0:T(8,128)(2,1)}), bf16[16,128,128]{2,1,0:T(8,128)(2,1)}, u32[]{:S(2)}, u32[]{:S(2)}) async-start(bf16[16,128,128]{2,1,0:T(8,128)(2,1)} %copy.76), calls=%async_computation.4 | async-start | bytes 1048576 | tf_op jit(solution)/shard_map/all_to_all | solution.py:23
  261.5 6.7 %convert_bitcast_fusion = bf16[1,2048,3072]{2,1,0:T(8,128)(2,1)} fusion(bf16[256,3072]{1,0:T(8,128)(2,1)S(1)} %copy-done.13, f32[256,2048]{1,0:T(8,128)S(1)} %copy-done.2, f32[2048]{0:T(1024)S(1)} %convert_element_type.75, f32[256]{0:T(256)S(1)} %bitcast.129), kind=kOutput, calls=%fused_computation | convolution fusion | flops 3229089792 | bytes 16262144 | tf_op jit(solution)/shard_map/dot_general | solution.py:68
  268.2 4.8 %all-to-all-done.3 = bf16[16,128,128]{2,1,0:T(8,128)(2,1)} async-done(((bf16[16,128,128]{2,1,0:T(8,128)(2,1)}), bf16[16,128,128]{2,1,0:T(8,128)(2,1)}, u32[]{:S(2)}, u32[]{:S(2)}) %all-to-all-start.3) | async-done | bytes 524320 | tf_op jit(solution)/shard_map/all_to_all | solution.py:23
  273.0 2.9 add_convert_fusion
  275.9 2.4 copy.84
  278.2 2.2 fusion
  (56 shorter events, 25.0 us)
Async XLA Ops:
  7.2 45.9 %copy-start = (bf16[256,2048]{1,0:T(8,128)(2,1)S(1)}, bf16[256,2048]{1,0:T(8,128)(2,1)}, u32[]{:S(2)}) copy-start(bf16[256,2048]{1,0:T(8,128)(2,1)} %param.6) | copy-start | bytes 3145732
  7.2 169.8 %all-gather.3.cloned.1.call-start = ((), (), s32[]{:S(2)}) async-start(), calls=%async_computation.5 | async-start | bytes 13369344 | tf_op jit(solution)/shard_map/all_gather | solution.py:52
  7.9 4.2 %copy-start.5 = (bf16[256,2048]{1,0:T(8,128)(2,1)S(1)}, bf16[256,2048]{1,0:T(8,128)(2,1)}, u32[]{:S(2)}) copy-start(bf16[256,2048]{1,0:T(8,128)(2,1)} %param.8) | copy-start | bytes 3145732
  12.1 31.4 %copy-start.3 = (bf16[256,16,128]{0,2,1:T(8,128)(2,1)}, bf16[256,16,128]{0,2,1:T(8,128)(2,1)S(1)}, u32[]{:S(2)}) copy-start(bf16[256,16,128]{0,2,1:T(8,128)(2,1)S(1)} %copy.59) | copy-start | bytes 3145732
  12.5 40.4 %copy-start.14 = (bf16[2048]{0:T(1024)(128)(2,1)S(1)}, bf16[2048]{0:T(1024)(128)(2,1)}, u32[]{:S(2)}) copy-start(bf16[2048]{0:T(1024)(128)(2,1)} %param.9) | copy-start | bytes 12292
  44.4 28.0 %all-to-all-start.1 = ((bf16[16,128,128]{2,1,0:T(8,128)(2,1)}), bf16[16,128,128]{2,1,0:T(8,128)(2,1)S(1)}, u32[]{:S(2)}, u32[]{:S(2)}) async-start(bf16[16,128,128]{2,1,0:T(8,128)(2,1)} %copy.62), calls=%async_computation.1 | async-start | bytes 1048576 | tf_op jit(solution)/shard_map/all_to_all | solution.py:23
  52.9 145.5 %reduce-scatter.2.cloned.1.call-start = ((), (), s32[]{:S(2)}) async-start(), calls=%async_computation.6 | async-start | bytes 2359296 | tf_op jit(solution)/shard_map/reduce_scatter | solution.py:54
  55.0 1.3 copy-start.8
  72.4 3.6 %copy-start.11 = (bf16[16,128,128]{2,1,0:T(8,128)(2,1)}, bf16[16,128,128]{2,1,0:T(8,128)(2,1)S(1)}, u32[]{:S(2)}) copy-start(bf16[16,128,128]{2,1,0:T(8,128)(2,1)S(1)} %all-to-all-done.1) | copy-start | bytes 1572868
  78.0 134.2 %copy-start.1 = (f32[256,2048]{1,0:T(8,128)}, f32[256,2048]{1,0:T(8,128)S(1)}, u32[]{:S(2)}) copy-start(f32[256,2048]{1,0:T(8,128)S(1)} %copy.65) | copy-start | bytes 6291460
  191.1 21.1 %all-gather.5.cloned.1.call-start = ((), (), s32[]{:S(2)}) async-start(), calls=%async_computation.7 | async-start | bytes 2359296 | tf_op jit(solution)/shard_map/all_gather | solution.py:59
  222.6 2.8 copy-start.6
  227.5 9.0 %copy-start.4 = (bf16[256,16,128]{0,2,1:T(8,128)(2,1)S(1)}, bf16[256,16,128]{0,2,1:T(8,128)(2,1)}, u32[]{:S(2)}) copy-start(bf16[256,16,128]{0,2,1:T(8,128)(2,1)} %copy-done.3) | copy-start | bytes 3145732
  229.7 22.4 %all-to-all-start.2 = ((bf16[16,128,128]{2,1,0:T(8,128)(2,1)}), bf16[16,128,128]{2,1,0:T(8,128)(2,1)}, u32[]{:S(2)}, u32[]{:S(2)}) async-start(bf16[16,128,128]{2,1,0:T(8,128)(2,1)} %copy.74), calls=%async_computation.3 | async-start | bytes 1048576 | tf_op jit(solution)/shard_map/all_to_all | solution.py:16
  236.5 2.5 copy-start.12
  244.2 14.4 %copy-start.9 = (bf16[16,256,256]{2,1,0:T(8,128)(2,1)S(1)}, bf16[16,256,256]{2,1,0:T(8,128)(2,1)}, u32[]{:S(2)}) copy-start(bf16[16,256,256]{2,1,0:T(8,128)(2,1)} %select_convert_fusion) | copy-start | bytes 6291460
  254.4 18.6 %all-to-all-start.3 = ((bf16[16,128,128]{2,1,0:T(8,128)(2,1)}), bf16[16,128,128]{2,1,0:T(8,128)(2,1)}, u32[]{:S(2)}, u32[]{:S(2)}) async-start(bf16[16,128,128]{2,1,0:T(8,128)(2,1)} %copy.76), calls=%async_computation.4 | async-start | bytes 1048576 | tf_op jit(solution)/shard_map/all_to_all | solution.py:23
  258.7 1.9 copy-start.2
  258.7 2.8 copy-start.13
  261.5 11.5 %copy-start.10 = (f32[16,128,256]{2,1,0:T(8,128)S(1)}, f32[16,128,256]{2,1,0:T(8,128)}, u32[]{:S(2)}) copy-start(f32[16,128,256]{2,1,0:T(8,128)} %fusion.34) | copy-start | bytes 6291460
  275.9 2.4 copy-start.7
Sparse Core Ops, SparseCore 0:
  10.8 166.2 all-gather.2
  191.2 7.1 reduce-scatter.1
  201.0 11.0 all-gather.4

commit v2 on v1

--- a/solution.py
+++ b/solution.py
@@ -1,6 +1,10 @@
+import functools
+
 import jax
 import jax.numpy as jnp
 from jax import lax
+from jax.experimental import pallas as pl
+from jax.experimental.pallas import tpu as pltpu
 from jax.sharding import PartitionSpec as P
 
 HEAD_DIM = 128
@@ -29,6 +33,328 @@
     return row_index >= col_index
 
 
+def remote(src, dst, send_sem, recv_sem, peer):
+    return pltpu.make_async_remote_copy(
+        src_ref=src,
+        dst_ref=dst,
+        send_sem=send_sem,
+        recv_sem=recv_sem,
+        device_id={"seq": peer},
+        device_id_type=pl.DeviceIdType.MESH,
+    )
+
+
+def exchange(count, me, source, target, send_sem, recv_sem):
+    def start(step, carry):
+        peer = lax.rem(me + step, count)
+        remote(source.at[peer], target.at[me], send_sem.at[step], recv_sem.at[step], peer).start()
+        return carry
+
+    lax.fori_loop(1, count, start, 0)
+    target[me] = source[me]
+
+
+def exchange_wait(count, me, source, target, send_sem, recv_sem):
+    def wait(step, carry):
+        peer = lax.rem(me + step, count)
+        origin = lax.rem(me - step + count, count)
+        remote(source.at[peer], target.at[origin], send_sem.at[step], recv_sem.at[step], peer).wait()
+        return carry
+
+    lax.fori_loop(1, count, wait, 0)
+
+
+def greet(count, me):
+    barrier = pltpu.get_barrier_semaphore()
+
+    def signal(step, carry):
+        pl.semaphore_signal(
+            barrier,
+            inc=1,
+            device_id={"seq": lax.rem(me + step, count)},
+            device_id_type=pl.DeviceIdType.MESH,
+        )
+        return carry
+
+    lax.fori_loop(1, count, signal, 0)
+    pl.semaphore_wait(barrier, count - 1)
+
+
+def running_sums(count, source, target, backward):
+    def one(step, total):
+        index = count - 1 - step if backward else step
+        target[index] = total.astype(jnp.bfloat16)
+        return total + source[index].astype(jnp.float32)
+
+    lax.fori_loop(0, count, one, jnp.zeros(source.shape[1:], jnp.float32))
+
+
+def columns_of(head):
+    return pl.ds(pl.multiple_of(head * HEAD_DIM, HEAD_DIM), HEAD_DIM)
+
+
+def pieces_of(head, per_head):
+    return pl.ds(head * per_head, per_head)
+
+
+def dims(left, right):
+    return (((left,), (right,)), ((), ()))
+
+
+def forward_kernel(
+    count,
+    q_ref,
+    k_ref,
+    v_ref,
+    w_ref,
+    full_ref,
+    mixed_ref,
+    scores_ref,
+    state_ref,
+    mine_ref,
+    spread_ref,
+    sums_ref,
+    x_sem,
+    y_sem,
+    up_sem,
+    down_sem,
+    land_sem,
+    first_send,
+    first_recv,
+    second_send,
+    second_recv,
+    own_sem,
+):
+    f32 = jnp.float32
+    me = lax.axis_index("seq")
+    layers = count // 4
+    layer, plane = me // 4, lax.rem(me, 4)
+    row, col = plane // 2, lax.rem(plane, 2)
+    plane_x = row * 2 + (1 - col)
+    plane_y = (1 - row) * 2 + col
+    plane_d = (1 - row) * 2 + (1 - col)
+    x_peer = layer * 4 + plane_x
+    y_peer = layer * 4 + plane_y
+    features = w_ref.shape[1]
+    blocks = features // 128
+    cut_a = blocks // 4
+    cut_b = cut_a + (blocks - cut_a + 1) // 2
+    edges = (0, cut_a * 128, cut_b * 128, features)
+    piece = [pl.ds(edges[i], edges[i + 1] - edges[i]) for i in range(3)]
+    local_heads = features // HEAD_DIM
+    per_head = HEAD_DIM // mine_ref.shape[1]
+    tok_count = q_ref.shape[0]
+
+    def copy(shard, part, send_sem, peer, own=False):
+        src = w_ref.at[:, piece[part]] if own else full_ref.at[shard, :, piece[part]]
+        return remote(
+            src, full_ref.at[shard, :, piece[part]], send_sem, land_sem.at[shard, part], peer
+        )
+
+    def landed(shard, part):
+        copy(shard, part, x_sem.at[layers, 2], x_peer).wait_recv()
+
+    def to_x(at, slot, shard, part, own=False):
+        return copy(shard, part, x_sem.at[at, slot], x_peer, own)
+
+    def to_y(at, slot, shard, part, own=False):
+        return copy(shard, part, y_sem.at[at, slot], y_peer, own)
+
+    def vertical(up, at, slot, shard, part, act, own=False, slack=None):
+        sem, peer = (up_sem, me + 4) if up else (down_sem, me - 4)
+        room = layers - 2 - layer if up else layer - 1
+        room = room if slack is None else jnp.minimum(room, slack)
+
+        @pl.when(room >= 0)
+        def _():
+            act(copy(shard, part, sem.at[at, slot], peer, own))
+
+    def begin(transfer):
+        transfer.start()
+
+    def finish(transfer):
+        transfer.wait_send()
+
+    def own_sends(act):
+        for part in (1, 2):
+            for up in (True, False):
+                vertical(up, layer, part - 1, me, part, act, True)
+            act(to_x(layer, part - 1, me, part, True))
+            act(to_y(layer, part - 1, me, part, True))
+        act(to_x(layers, 0, me, 0, True))
+        act(to_y(layers, 0, me, 0, True))
+        for up in (True, False):
+            vertical(up, layer, 2 + 0, me, 0, act, True)
+
+    def sources(step):
+        if step == 0:
+            return ((layer, None, None),)
+        return (
+            (layer - step, layer - step, True),
+            (layer + step, layers - 1 - layer - step, False),
+        )
+
+    def column_step(step, act, waiting):
+        for at, slack, up in sources(step):
+            shard = at * 4 + plane
+            for part in (1, 2):
+
+                @pl.when(slack >= 0)
+                def _():
+                    if waiting:
+                        landed(shard, part)
+                    act(to_x(at, part - 1, shard, part))
+                    act(to_y(at, part - 1, shard, part))
+
+                vertical(up, at, part - 1, shard, part, act, slack=slack)
+
+    def guarded(slack, body):
+        if slack is None:
+            body()
+        else:
+            pl.when(slack >= 0)(body)
+
+    def diagonal_step(step, act, waiting):
+        for at, slack, _unused in sources(step):
+
+            def body(at=at):
+                if waiting:
+                    landed(at * 4 + plane_y, 1)
+                act(to_x(at, 2, at * 4 + plane_y, 1))
+                if waiting:
+                    landed(at * 4 + plane_x, 2)
+                act(to_y(at, 2, at * 4 + plane_x, 2))
+
+            guarded(slack, body)
+
+    others = (plane_x, plane_y, plane_d)
+
+    def plane_step(act, waiting):
+        for slot, other in enumerate(others):
+            shard = layer * 4 + other
+            if waiting:
+                landed(shard, 0)
+            if slot == 0:
+                act(to_y(layers, 1, shard, 0))
+            for up in (True, False):
+                vertical(up, layer, 3 + slot, shard, 0, act)
+
+    def plane_chain(step, act, waiting):
+        for at, slack, up in sources(step):
+            for slot, other in enumerate((plane,) + others):
+                shard = at * 4 + other
+                if waiting:
+
+                    @pl.when(slack >= 0)
+                    def _():
+                        landed(shard, 0)
+
+                vertical(up, at, 2 + slot, shard, 0, act, slack=slack)
+
+    greet(count, me)
+    own_sends(begin)
+    own = pltpu.make_async_copy(w_ref, full_ref.at[me], own_sem)
+    own.start()
+
+    def outer(head, carry):
+        cols = columns_of(head)
+        state = lax.dot_general(
+            k_ref[:, cols], v_ref[:, cols], dims(0, 0), preferred_element_type=f32
+        )
+        state = state.reshape((per_head,) + mine_ref.shape[1:])
+        mine_ref[pieces_of(head, per_head)] = state.astype(jnp.bfloat16)
+        return carry
+
+    lax.fori_loop(0, local_heads, outer, 0)
+    exchange(count, me, mine_ref, spread_ref, first_send, first_recv)
+    keep = causal(tok_count)
+
+    def inside(head, carry):
+        cols = columns_of(head)
+        scores = lax.dot_general(
+            q_ref[:, cols], k_ref[:, cols], dims(1, 1), preferred_element_type=f32
+        )
+        scores = jnp.where(keep, scores, 0.0).astype(jnp.bfloat16)
+        scores_ref[head] = scores
+        mixed_ref[:, cols] = jnp.dot(scores, v_ref[:, cols], preferred_element_type=f32)
+        return carry
+
+    lax.fori_loop(0, local_heads, inside, 0)
+    column_step(1, begin, True)
+    diagonal_step(0, begin, True)
+    plane_step(begin, True)
+    exchange_wait(count, me, mine_ref, spread_ref, first_send, first_recv)
+    running_sums(count, spread_ref, sums_ref, False)
+    exchange(count, me, sums_ref, state_ref, second_send, second_recv)
+    for step in range(2, layers):
+        column_step(step, begin, True)
+        diagonal_step(step - 1, begin, True)
+        plane_chain(step - 1, begin, True)
+    exchange_wait(count, me, sums_ref, state_ref, second_send, second_recv)
+
+    def across(head, carry):
+        cols = columns_of(head)
+        state = state_ref[pieces_of(head, per_head)].reshape(HEAD_DIM, HEAD_DIM)
+        mixed_ref[:, cols] += jnp.dot(q_ref[:, cols], state, preferred_element_type=f32)
+        return carry
+
+    lax.fori_loop(0, local_heads, across, 0)
+    diagonal_step(layers - 1, begin, True)
+    plane_chain(layers - 1, begin, True)
+    for at in range(layers):
+        landed(at * 4 + plane_x, 1)
+        landed(at * 4 + plane_y, 2)
+        landed(at * 4 + plane_d, 1)
+        landed(at * 4 + plane_d, 2)
+    own_sends(finish)
+    plane_step(finish, False)
+    diagonal_step(0, finish, False)
+    for step in range(1, layers):
+        column_step(step, finish, False)
+        diagonal_step(step, finish, False)
+        plane_chain(step, finish, False)
+    own.wait()
+
+
+def forward_part(queries, key_input, value_input, weight):
+    count = lax.axis_size("seq")
+    tok_count, features = queries.shape
+    local_heads = features // HEAD_DIM
+    layers = count // 4
+    piece_shape = (count, local_heads * HEAD_DIM // count, HEAD_DIM)
+    low = jnp.bfloat16
+    vmem = pl.BlockSpec(memory_space=pltpu.VMEM)
+    dma = pltpu.SemaphoreType.DMA
+    return pl.pallas_call(
+        functools.partial(forward_kernel, count),
+        out_shape=(
+            jax.ShapeDtypeStruct((count,) + weight.shape, low),
+            jax.ShapeDtypeStruct((tok_count, features), jnp.float32),
+            jax.ShapeDtypeStruct((local_heads, tok_count, tok_count), low),
+            jax.ShapeDtypeStruct(piece_shape, low),
+        ),
+        in_specs=[vmem] * 4,
+        out_specs=(pl.BlockSpec(memory_space=pl.ANY), vmem, vmem, vmem),
+        scratch_shapes=[
+            pltpu.VMEM(piece_shape, low),
+            pltpu.VMEM(piece_shape, low),
+            pltpu.VMEM(piece_shape, low),
+            dma((layers + 1, 3)),
+            dma((layers + 1, 3)),
+            dma((layers, 6)),
+            dma((layers, 6)),
+            dma((count, 3)),
+            dma((count,)),
+            dma((count,)),
+            dma((count,)),
+            dma((count,)),
+            dma(()),
+        ],
+        compiler_params=pltpu.CompilerParams(collective_id=0, has_side_effects=True),
+        name="forward_part",
+    )(queries, key_input, value_input, weight)
+
+
 def per_device(queries, key_input, value_input, norm_gain, out_weight, target):
     tok_count = queries.shape[0]
     local_heads = queries.shape[1] // HEAD_DIM
@@ -38,19 +364,18 @@
     v_heads = value_input.reshape(shape3)
     keep_mask = causal(tok_count)
     f32 = jnp.float32
-    state_local = jnp.einsum("shd,she->hde", k_heads, v_heads, preferred_element_type=f32)
-    state_low = entering(state_local, "seq", False)
-    scores = jnp.einsum("thd,shd->hts", q_heads, k_heads, preferred_element_type=f32)
-    scores_low = jnp.where(keep_mask[None], scores, 0.0).astype(jnp.bfloat16)
-    attended = jnp.einsum("hts,shd->thd", scores_low, v_heads, preferred_element_type=f32)
-    attended = attended + jnp.einsum("thd,hde->the", q_heads, state_low, preferred_element_type=f32)
-    mixed = attended.reshape(tok_count, -1)
+    gathered, mixed, scores_low, state_low = forward_part(
+        queries, key_input, value_input, out_weight.T
+    )
+    state_low = state_low.reshape(local_heads, HEAD_DIM, HEAD_DIM)
+    full_weight = gathered.reshape(-1, gathered.shape[2])
     gain_float = norm_gain.astype(f32)
     squares = lax.psum(jnp.sum(mixed * mixed, axis=1, keepdims=True), "head")
     inverse = lax.rsqrt(squares / FEATURES + EPSILON)
     normed = (mixed * inverse * gain_float).astype(jnp.bfloat16)
-    full_weight = lax.all_gather(out_weight, "seq", axis=1, tiled=True)
-    partial_value = jnp.dot(normed, full_weight, preferred_element_type=f32)
+    partial_value = lax.dot_general(
+        normed, full_weight, (((1,), (1,)), ((), ())), preferred_element_type=f32
+    )
     projected = lax.psum_scatter(
         partial_value.astype(jnp.bfloat16), "head", scatter_dimension=1, tiled=True
     ).astype(jnp.float32)
@@ -58,7 +383,7 @@
     grad_local = (projected - target.astype(f32)).astype(jnp.bfloat16)
     out_grad = lax.all_gather(grad_local, "head", axis=1, tiled=True)
     normed_grad = lax.dot_general(
-        out_grad, full_weight, (((1,), (1,)), ((), ())), preferred_element_type=f32
+        out_grad, full_weight, (((1,), (0,)), ((), ())), preferred_element_type=f32
     )
     product = jnp.sum(grad_local.astype(f32) * projected, axis=1, keepdims=True)
     inner = lax.psum(product, "head") / inverse

time: 289 us -> 255 us (0.88)
  Pallas kernels: 0 us -> 132 us
  waiting for transfers between devices: 140 us -> 24.6 us
  blocking collectives: 35.6 us -> 4.94 us
  starting transfers between devices: 19.7 us -> 11.2 us
  local copies, waits for them, and re-layouts: 19.1 us -> 11.2 us
  matrix products: 57.7 us -> 51.7 us
    pallas_call x0 -> x1, Pallas kernels: none -> 132 us  [forward_part(): pl.pallas_call(functools.partial(forward_kernel, count), out_shape=(jax.S...]
    all_gather x1 -> x0, waiting for transfers between devices: 96.6 us -> none  [per_device(): full_weight = lax.all_gather(out_weight, 'seq', axis=1, tiled=True)]
    all_to_all x1 -> x0, blocking collectives: 30.5 us -> none  [entering(): spread = lax.all_to_all(pieces, axis, 0, 0)]
    all_to_all x2 -> x1, waiting for transfers between devices: 18.8 us -> 4.16 us  [entering(): lax.all_to_all(sums.astype(jnp.bfloat16), axis, 0, 0).reshape(shard.shape)]
    all_to_all x2 -> x1, starting transfers between devices: 12.7 us -> 4.24 us  [entering(): lax.all_to_all(sums.astype(jnp.bfloat16), axis, 0, 0).reshape(shard.shape)]
    dot_general x6 -> x2, matrix products: 32.6 us -> 24.5 us  [the longest x1 14.1 us: per_device(): lax.dot_general(normed, full_weight, (((1,), (1,)), ((), ())), preferred_...]
    reshape x2 -> x0, local copies, waits for them, and re-layouts: 3.55 us -> none  [the longest x1 1.92 us: per_device(): mixed = attended.reshape(tok_count, -1)]
    unnamed x34 -> x21, local copies, waits for them, and re-layouts: 10 us -> 6.72 us
  transfers between devices with their start and end apart: 6 -> 4, of which waited for: 6 -> 4; matrix products, arithmetic and copies ran while one was open for 11% -> 8% of each run, Pallas kernels for 0% -> 0%
where the time goes in v2:
time: 255 us; the launch traced here: 254 us
  Pallas kernels  132 us (52%)
  matrix products  51.7 us (20%)
  waiting for transfers between devices  24.6 us (10%)
  between operations  14.2 us (6%)
  starting transfers between devices  11.2 us (4%)
  local copies, waits for them, and re-layouts  11.2 us (4%)
  blocking collectives  4.94 us (2%)
  other arithmetic  4.3 us (2%)
    pallas_call x1, Pallas kernels, forward_part(): pl.pallas_call(functools.partial(forward_kernel, count), out_shape=(jax.S...  132 us
    dot_general x1, matrix products, per_device(): lax.dot_general(normed, full_weight, (((1,), (1,)), ((), ())), preferred_...  14.1 us
    dot_general x1, matrix products, per_device(): lax.dot_general(out_grad, full_weight, (((1,), (0,)), ((), ())), preferre...  10.4 us
    all_gather x1, waiting for transfers between devices, per_device(): out_grad = lax.all_gather(grad_local, 'head', axis=1, tiled=True)  8.71 us
    reduce_scatter x1, waiting for transfers between devices, per_device(): lax.psum_scatter(partial_value.astype(jnp.bfloat16), 'head', scatter_dime...  7.15 us
    all_to_all x1, starting transfers between devices, entering(): spread = lax.all_to_all(pieces, axis, 0, 0)  6.86 us
    unnamed x21, local copies, waits for them, and re-layouts  6.72 us
    dot_general x1, matrix products, per_device(): lax.dot_general(normed, out_grad, (((0,), (0,)), ((), ())), preferred_ele...  6.7 us
  transfers between devices with their start and end apart: 4, of which 4 were waited for; matrix products, arithmetic and copies ran while one was open for 8% of the time, Pallas kernels for 0%

profile of v2, /device:TPU:0, one launch (start us, length us, event | category | flops | bytes accessed | tf_op | source)
XLA Modules:
  0.0 254.1 jit_solution(10084915930291145883)
XLA Ops:
  7.2 132.0 %forward_part.1 = (bf16[16,192,2048]{2,1,0:T(8,128)(2,1)}, f32[256,2048]{1,0:T(8,128)}, bf16[16,256,256]{2,1,0:T(8,128)(2,1)}, bf16[16,128,128]{2,1,0:T(8,128)(2,1)}) custom-call(bf16[256,2048]{1,0:T(8,128)(2,1)} %q_ref.1, bf16[256,2048]{1,0:T(8,128)(2,1)} %k_ref.1, bf16[256,2048]{1,0:T(8,128)(2,1)} %v_ref.1, bf16[192,2048]{1,0:T(8,128)(2,1)} %bitcast.90), custom_call_target="tpu_custom_call" | custom-call | tf_op jit(solution)/shard_map/forward_part/pallas_call | solution.py:328
  139.3 2.0 multiply_reduce_fusion.1
  141.2 2.5 psum.14
  143.8 14.1 %convolution_convert_fusion = bf16[256,3072]{1,0:T(8,128)(2,1)} fusion(bf16[3072,2048]{1,0:T(8,128)(2,1)} %bitcast.98, f32[256,2048]{1,0:T(8,128)S(1)} %copy-done, f32[2048]{0:T(1024)S(1)} %convert_element_type.62, f32[256]{0:T(256)S(1)} %bitcast.91), kind=kOutput, calls=%fused_computation.2 | convolution fusion | flops 3223584768 | bytes 16262144 | tf_op jit(solution)/shard_map/dot_general | solution.py:376
  157.9 7.2 %reduce-scatter.2.cloned.1.call-done = bf16[256,1536]{1,0:T(8,128)(2,1)} async-done(((bf16[256,3072]{1,0:T(8,128)(2,1)}), bf16[256,1536]{1,0:T(8,128)(2,1)}) %reduce-scatter.2.cloned.1.call-update) | async-done | bytes 786448 | tf_op jit(solution)/shard_map/reduce_scatter | solution.py:379
  165.1 2.3 fusion.3
  167.4 2.5 psum.15
  169.9 8.7 %all-gather.2.cloned.1.call-done = bf16[256,3072]{1,0:T(8,128)(2,1)} async-done(((bf16[256,1536]{1,0:T(8,128)(2,1)}), bf16[256,3072]{1,0:T(8,128)(2,1)}) %all-gather.2.cloned.1.call-update) | async-done | bytes 1572880 | tf_op jit(solution)/shard_map/all_gather | solution.py:384
  178.6 10.4 %multiply_reduce_fusion = (f32[2048]{0:T(1024)}, bf16[256,2048]{1,0:T(8,128)(2,1)}) fusion(f32[256,2048]{1,0:T(8,128)S(1)} %copy-done, f32[256]{0:T(256)S(1)} %bitcast.92, f32[256]{0:T(256)S(1)} %bitcast.97, f32[256]{0:T(256)S(1)} %bitcast.96, f32[2048]{0:T(1024)S(1)} %convert_element_type.62, bf16[256,3072]{1,0:T(8,128)(2,1)} %all-gather.2.cloned.1.call-done, ...), kind=kOutput, calls=%fused_computation.7 | convolution fusion | flops 3226466304 | bytes 17320960 | tf_op jit(solution)/shard_map/dot_general | solution.py:385
  189.0 1.5 copy.56
  190.5 2.4 fusion.4
  192.9 2.0 copy.45
  195.0 6.9 %all-to-all-start = ((bf16[16,128,128]{2,1,0:T(8,128)(2,1)}), bf16[16,128,128]{2,1,0:T(8,128)(2,1)}, u32[]{:S(2)}, u32[]{:S(2)}) async-start(bf16[16,128,128]{2,1,0:T(8,128)(2,1)} %copy.45), calls=%async_computation.1 | async-start | bytes 1048576 | tf_op jit(solution)/shard_map/all_to_all | solution.py:20
  201.9 2.1 select_convert_fusion
  206.8 2.3 copy.52
  209.1 3.8 %fusion.5 = f32[16,256,128]{1,2,0:T(8,128)} fusion(bf16[16,256,256]{2,1,0:T(8,128)(2,1)} %copy-done.4, bf16[256,2048]{1,0:T(8,128)(2,1)} %q_ref.1), kind=kOutput, calls=%fused_computation.19 | convolution fusion | flops 268435456 | bytes 5242880 | tf_op jit(solution)/shard_map/hts,thd->shd/dot_general | solution.py:405
  212.9 4.5 %all-to-all-done = bf16[16,128,128]{2,1,0:T(8,128)(2,1)} async-done(((bf16[16,128,128]{2,1,0:T(8,128)(2,1)}), bf16[16,128,128]{2,1,0:T(8,128)(2,1)}, u32[]{:S(2)}, u32[]{:S(2)}) %all-to-all-start) | async-done | bytes 524320 | tf_op jit(solution)/shard_map/all_to_all | solution.py:20
  219.8 4.2 %all-to-all-start.1 = ((bf16[16,128,128]{2,1,0:T(8,128)(2,1)}), bf16[16,128,128]{2,1,0:T(8,128)(2,1)}, u32[]{:S(2)}, u32[]{:S(2)}) async-start(bf16[16,128,128]{2,1,0:T(8,128)(2,1)} %copy.47), calls=%async_computation.2 | async-start | bytes 1048576 | tf_op jit(solution)/shard_map/all_to_all | solution.py:27
  224.0 3.5 %fusion.22 = f32[16,128,256]{2,1,0:T(8,128)} fusion(bf16[256,16,128]{0,2,1:T(8,128)(2,1)S(1)} %bitcast.86, bf16[16,256,256]{2,1,0:T(8,128)(2,1)} %get-tuple-element.13), kind=kOutput, calls=%fused_computation.39 | convolution fusion | flops 268435456 | bytes 5242880 | tf_op jit(solution)/shard_map/hts,the->she/dot_general | solution.py:407
  227.5 6.7 %convert_bitcast_fusion = bf16[1,2048,3072]{2,1,0:T(8,128)(2,1)} fusion(bf16[256,3072]{1,0:T(8,128)(2,1)S(1)} %copy-done.5, f32[256,2048]{1,0:T(8,128)S(1)} %copy-done, f32[2048]{0:T(1024)S(1)} %convert_element_type.62, f32[256]{0:T(256)S(1)} %bitcast.93), kind=kOutput, calls=%fused_computation | convolution fusion | flops 3229089792 | bytes 16262144 | tf_op jit(solution)/shard_map/dot_general | solution.py:393
  234.2 4.2 %all-to-all-done.1 = bf16[16,128,128]{2,1,0:T(8,128)(2,1)} async-done(((bf16[16,128,128]{2,1,0:T(8,128)(2,1)}), bf16[16,128,128]{2,1,0:T(8,128)(2,1)}, u32[]{:S(2)}, u32[]{:S(2)}) %all-to-all-start.1) | async-done | bytes 524320 | tf_op jit(solution)/shard_map/all_to_all | solution.py:27
  238.3 3.2 %add_convert_fusion = bf16[16,128,256]{2,1,0:T(8,128)(2,1)} fusion(f32[16,128,256]{2,1,0:T(8,128)} %fusion.22, bf16[16,128,128]{2,1,0:T(8,128)(2,1)} %all-to-all-done.1, bf16[256,2048]{1,0:T(8,128)(2,1)S(1)} %copy-done.2), kind=kOutput, calls=%fused_computation.8 | convolution fusion | flops 135266304 | bytes 4718592 | tf_op jit(solution)/shard_map/shd,hde->she/dot_general | solution.py:408
  241.6 2.4 copy.54
  244.0 1.8 fusion
  (31 shorter events, 6.8 us)
Async XLA Ops:
  7.2 157.9 %reduce-scatter.2.cloned.1.call-start = ((), (), s32[]{:S(2)}) async-start(), calls=%async_computation.3 | async-start | bytes 2359296 | tf_op jit(solution)/shard_map/reduce_scatter | solution.py:379
  7.2 136.5 %copy-start.8 = (bf16[2048]{0:T(1024)(128)(2,1)S(1)}, bf16[2048]{0:T(1024)(128)(2,1)}, u32[]{:S(2)}) copy-start(bf16[2048]{0:T(1024)(128)(2,1)} %param.9) | copy-start | bytes 12292
  139.3 4.5 %copy-start = (f32[256,2048]{1,0:T(8,128)S(1)}, f32[256,2048]{1,0:T(8,128)}, u32[]{:S(2)}) copy-start(f32[256,2048]{1,0:T(8,128)} %get-tuple-element.10) | copy-start | bytes 6291460
  157.8 7.2 %copy-start.6 = (bf16[256,1536]{1,0:T(8,128)(2,1)S(1)}, bf16[256,1536]{1,0:T(8,128)(2,1)}, u32[]{:S(2)}) copy-start(bf16[256,1536]{1,0:T(8,128)(2,1)} %param.11) | copy-start | bytes 2359300
  157.8 20.7 %all-gather.2.cloned.1.call-start = ((), (), s32[]{:S(2)}) async-start(), calls=%async_computation.4 | async-start | bytes 2359296 | tf_op jit(solution)/shard_map/all_gather | solution.py:384
  195.0 22.4 %all-to-all-start = ((bf16[16,128,128]{2,1,0:T(8,128)(2,1)}), bf16[16,128,128]{2,1,0:T(8,128)(2,1)}, u32[]{:S(2)}, u32[]{:S(2)}) async-start(bf16[16,128,128]{2,1,0:T(8,128)(2,1)} %copy.45), calls=%async_computation.1 | async-start | bytes 1048576 | tf_op jit(solution)/shard_map/all_to_all | solution.py:20
  201.9 2.1 copy-start.1
  204.0 1.3 copy-start.4
  204.0 1.4 copy-start.7
  219.8 18.6 %all-to-all-start.1 = ((bf16[16,128,128]{2,1,0:T(8,128)(2,1)}), bf16[16,128,128]{2,1,0:T(8,128)(2,1)}, u32[]{:S(2)}, u32[]{:S(2)}) async-start(bf16[16,128,128]{2,1,0:T(8,128)(2,1)} %copy.47), calls=%async_computation.2 | async-start | bytes 1048576 | tf_op jit(solution)/shard_map/all_to_all | solution.py:27
  224.0 3.5 %copy-start.5 = (bf16[256,3072]{1,0:T(8,128)(2,1)S(1)}, bf16[256,3072]{1,0:T(8,128)(2,1)}, u32[]{:S(2)}) copy-start(bf16[256,3072]{1,0:T(8,128)(2,1)} %all-gather.2.cloned.1.call-done) | copy-start | bytes 4718596
  227.5 10.9 %copy-start.2 = (bf16[256,2048]{1,0:T(8,128)(2,1)S(1)}, bf16[256,2048]{1,0:T(8,128)(2,1)}, u32[]{:S(2)}) copy-start(bf16[256,2048]{1,0:T(8,128)(2,1)} %k_ref.1) | copy-start | bytes 3145732
  241.6 2.4 copy-start.3
Sparse Core Ops, SparseCore 0:
  158.0 7.0 reduce-scatter.1
  167.5 11.0 all-gather.1

commit v3 on v2

--- a/solution.py
+++ b/solution.py
@@ -14,32 +14,19 @@
 EPSILON = 1e-06
 
 
-def entering(shard, axis, backward):
-    count = lax.axis_size(axis)
-    pieces = shard.astype(jnp.bfloat16).reshape(count, -1, shard.shape[-1])
-    spread = lax.all_to_all(pieces, axis, 0, 0)
-    row_index = lax.broadcasted_iota(jnp.int32, (count, count), 0)
-    col_index = lax.broadcasted_iota(jnp.int32, (count, count), 1)
-    chosen = col_index > row_index if backward else col_index < row_index
-    sums = jnp.einsum(
-        "ij,jrc->irc", chosen.astype(jnp.bfloat16), spread, preferred_element_type=jnp.float32
-    )
-    return lax.all_to_all(sums.astype(jnp.bfloat16), axis, 0, 0).reshape(shard.shape)
-
-
 def causal(count):
     row_index = lax.broadcasted_iota(jnp.int32, (count, count), 0)
     col_index = lax.broadcasted_iota(jnp.int32, (count, count), 1)
     return row_index >= col_index
 
 
-def remote(src, dst, send_sem, recv_sem, peer):
+def remote(src, dst, send_sem, recv_sem, peer, axis="seq"):
     return pltpu.make_async_remote_copy(
         src_ref=src,
         dst_ref=dst,
         send_sem=send_sem,
         recv_sem=recv_sem,
-        device_id={"seq": peer},
+        device_id={axis: peer},
         device_id_type=pl.DeviceIdType.MESH,
     )
 
@@ -64,20 +51,21 @@
     lax.fori_loop(1, count, wait, 0)
 
 
-def greet(count, me):
+def greet(*axes):
     barrier = pltpu.get_barrier_semaphore()
-
-    def signal(step, carry):
-        pl.semaphore_signal(
-            barrier,
-            inc=1,
-            device_id={"seq": lax.rem(me + step, count)},
-            device_id_type=pl.DeviceIdType.MESH,
-        )
-        return carry
-
-    lax.fori_loop(1, count, signal, 0)
-    pl.semaphore_wait(barrier, count - 1)
+    for axis, count, me in axes:
+
+        def signal(step, carry):
+            pl.semaphore_signal(
+                barrier,
+                inc=1,
+                device_id={axis: lax.rem(me + step, count)},
+                device_id_type=pl.DeviceIdType.MESH,
+            )
+            return carry
+
+        lax.fori_loop(1, count, signal, 0)
+    pl.semaphore_wait(barrier, sum(count - 1 for _unused, count, _unused2 in axes))
 
 
 def running_sums(count, source, target, backward):
@@ -251,7 +239,7 @@
 
                 vertical(up, at, 2 + slot, shard, 0, act, slack=slack)
 
-    greet(count, me)
+    greet(("seq", count, me))
     own_sends(begin)
     own = pltpu.make_async_copy(w_ref, full_ref.at[me], own_sem)
     own.start()
@@ -355,68 +343,306 @@
     )(queries, key_input, value_input, weight)
 
 
+def backward_kernel(
+    count,
+    groups,
+    mixed_ref,
+    gain_ref,
+    w_hbm,
+    target_ref,
+    q_ref,
+    k_ref,
+    v_ref,
+    scores_ref,
+    state_ref,
+    output_ref,
+    normed_ref,
+    out_grad_ref,
+    query_ref,
+    key_ref,
+    value_ref,
+    gain_grad_ref,
+    w_ref,
+    part_mine,
+    part_land,
+    own_part,
+    square_mine,
+    square_land,
+    product_mine,
+    product_land,
+    normed_grad_ref,
+    key_part,
+    mixed_grad_ref,
+    mine_ref,
+    spread_ref,
+    sums_ref,
+    later_ref,
+    w_sem,
+    head_send,
+    head_recv,
+    first_send,
+    first_recv,
+    second_send,
+    second_recv,
+):
+    f32 = jnp.float32
+    low = jnp.bfloat16
+    me = lax.axis_index("seq")
+    group = lax.axis_index("head")
+    tok_count, features = q_ref.shape
+    block = target_ref.shape[1]
+    tile = 256 if block % 256 == 0 else 128
+    wide = 256
+    local_heads = features // HEAD_DIM
+    per_head = HEAD_DIM // mine_ref.shape[1]
+    ahead = [lax.rem(group + step, groups) for step in range(groups)]
+    behind = [lax.rem(group + groups - step, groups) for step in range(groups)]
+
+    def block_rows(index):
+        return pl.ds(pl.multiple_of(index * block, block), block)
+
+    def tile_of(index, size, base=0):
+        return pl.ds(pl.multiple_of(base + index * size, size), size)
+
+    def w_copy(step):
+        rows = block_rows(ahead[step])
+        return pltpu.make_async_copy(w_hbm.at[rows], w_ref.at[rows], w_sem.at[step])
+
+    def head_copy(kind, step, src, dst):
+        return remote(
+            src, dst, head_send.at[kind, step], head_recv.at[kind, step], ahead[step], "head"
+        )
+
+    def square_copy(step):
+        return head_copy(0, step, square_mine, square_land.at[step])
+
+    def part_copy(step):
+        return head_copy(1, step, part_mine.at[step], part_land.at[step])
+
+    def product_copy(step):
+        return head_copy(2, step, product_mine, product_land.at[step])
+
+    def grad_copy(step, index):
+        cols = block_rows(index)
+        return head_copy(3, step, out_grad_ref.at[:, cols], out_grad_ref.at[:, cols])
+
+    order = list(range(1, groups)) + [0]
+    for step in order:
+        w_copy(step).start()
+    greet(("seq", count, me), ("head", groups, group))
+
+    def squared(index, total):
+        value = mixed_ref[:, tile_of(index, wide)]
+        return total + jnp.sum(value * value, axis=1, keepdims=True)
+
+    squares = lax.fori_loop(0, features // wide, squared, jnp.zeros((tok_count, 1), f32))
+    square_mine[...] = jnp.broadcast_to(squares, square_mine.shape)
+    for step in range(1, groups):
+        square_copy(step).start()
+    for step in range(1, groups):
+        square_copy(step).wait()
+        squares = squares + square_land[step][:, :1]
+    inverse = lax.rsqrt(squares / FEATURES + EPSILON)
+
+    def normalize(index, carry):
+        cols = tile_of(index, wide)
+        gain = gain_ref[:, cols].astype(f32)
+        normed_ref[:, cols] = (mixed_ref[:, cols] * inverse * gain).astype(low)
+        return carry
+
+    lax.fori_loop(0, features // wide, normalize, 0)
+
+    for step in order:
+        w_copy(step).wait()
+
+        def project(index, carry, step=step):
+            rows = tile_of(index, tile, ahead[step] * block)
+            value = lax.dot_general(
+                normed_ref[...], w_ref[rows, :], dims(1, 1), preferred_element_type=f32
+            )
+            if step:
+                part_mine[step, :, tile_of(index, tile)] = value.astype(low)
+            else:
+                own_part[:, tile_of(index, tile)] = value
+            return carry
+
+        lax.fori_loop(0, block // tile, project, 0)
+        if step:
+            part_copy(step).start()
+    for step in range(1, groups):
+        part_copy(step).wait()
+
+    def finish(index, total):
+        cols = tile_of(index, tile)
+        projected = own_part[:, cols]
+        for step in range(1, groups):
+            projected = projected + part_land[step, :, cols].astype(f32)
+        output_ref[:, cols] = projected.astype(low)
+        grad = (projected - target_ref[:, cols].astype(f32)).astype(low)
+        out_grad_ref[:, tile_of(index, tile, group * block)] = grad
+        return total + jnp.sum(grad.astype(f32) * projected, axis=1, keepdims=True)
+
+    product = lax.fori_loop(0, block // tile, finish, jnp.zeros((tok_count, 1), f32))
+    product_mine[...] = jnp.broadcast_to(product, product_mine.shape)
+    for step in range(1, groups):
+        grad_copy(step, group).start()
+        product_copy(step).start()
+
+    def first_grad(index, carry):
+        cols = tile_of(index, wide)
+        rows = block_rows(group)
+        normed_grad_ref[:, cols] = jnp.dot(
+            out_grad_ref[:, rows], w_ref[rows, cols], preferred_element_type=f32
+        )
+        return carry
+
+    lax.fori_loop(0, features // wide, first_grad, 0)
+    for step in range(1, groups):
+        grad_copy(step, group).wait_send()
+        grad_copy(step, behind[step]).wait_recv()
+        product_copy(step).wait()
+        product = product + product_land[step][:, :1]
+    inner = product / inverse
+    pull = inverse**3 * inner / FEATURES
+
+    def rest(index, carry):
+        cols = tile_of(index, wide)
+        grad = normed_grad_ref[:, cols]
+        for step in range(1, groups):
+            rows = block_rows(behind[step])
+            grad = grad + jnp.dot(
+                out_grad_ref[:, rows], w_ref[rows, cols], preferred_element_type=f32
+            )
+        mixed = mixed_ref[:, cols]
+        gain = gain_ref[:, cols].astype(f32)
+        gain_grad_ref[:, cols] = jnp.sum(grad * mixed * inverse, axis=0, keepdims=True)
+        mixed_grad = (inverse * gain * grad - mixed * pull).astype(low)
+        mixed_grad_ref[:, cols] = mixed_grad
+        for half in range(wide // HEAD_DIM):
+            head = index * (wide // HEAD_DIM) + half
+            state = lax.dot_general(
+                q_ref[:, columns_of(head)],
+                mixed_grad[:, half * HEAD_DIM : (half + 1) * HEAD_DIM],
+                dims(0, 0),
+                preferred_element_type=f32,
+            )
+            state = state.reshape((per_head,) + mine_ref.shape[1:])
+            mine_ref[pieces_of(head, per_head)] = state.astype(low)
+        return carry
+
+    lax.fori_loop(0, features // wide, rest, 0)
+    exchange(count, me, mine_ref, spread_ref, first_send, first_recv)
+    keep = causal(tok_count)
+
+    def inside(head, carry):
+        cols = columns_of(head)
+        grad = mixed_grad_ref[:, cols]
+        pairs = lax.dot_general(grad, v_ref[:, cols], dims(1, 1), preferred_element_type=f32)
+        pairs = jnp.where(keep, pairs, 0.0).astype(low)
+        state = state_ref[pieces_of(head, per_head)].reshape(HEAD_DIM, HEAD_DIM)
+        query = jnp.dot(pairs, k_ref[:, cols], preferred_element_type=f32)
+        query = query + lax.dot_general(grad, state, dims(1, 1), preferred_element_type=f32)
+        query_ref[:, cols] = query.astype(low)
+        key_part[:, cols] = lax.dot_general(
+            pairs, q_ref[:, cols], dims(0, 0), preferred_element_type=f32
+        )
+        return carry
+
+    def values(head, carry):
+        cols = columns_of(head)
+        normed_grad_ref[:, cols] = lax.dot_general(
+            scores_ref[head], mixed_grad_ref[:, cols], dims(0, 0), preferred_element_type=f32
+        )
+        return carry
+
+    lax.fori_loop(0, local_heads, inside, 0)
+    exchange_wait(count, me, mine_ref, spread_ref, first_send, first_recv)
+    running_sums(count, spread_ref, sums_ref, True)
+    exchange(count, me, sums_ref, later_ref, second_send, second_recv)
+    lax.fori_loop(0, local_heads, values, 0)
+    exchange_wait(count, me, sums_ref, later_ref, second_send, second_recv)
+
+    def last(head, carry):
+        cols = columns_of(head)
+        later = later_ref[pieces_of(head, per_head)].reshape(HEAD_DIM, HEAD_DIM)
+        key = lax.dot_general(v_ref[:, cols], later, dims(1, 1), preferred_element_type=f32)
+        key_ref[:, cols] = (key_part[:, cols] + key).astype(low)
+        value = jnp.dot(k_ref[:, cols], later, preferred_element_type=f32)
+        value_ref[:, cols] = (normed_grad_ref[:, cols] + value).astype(low)
+        return carry
+
+    lax.fori_loop(0, local_heads, last, 0)
+
+
+def backward_part(mixed, gain, weight, target, queries, key_input, value_input, scores, state):
+    count, groups = lax.axis_size("seq"), lax.axis_size("head")
+    tok_count, features = queries.shape
+    block = target.shape[1]
+    width = weight.shape[0]
+    low, f32 = jnp.bfloat16, jnp.float32
+    vmem = pl.BlockSpec(memory_space=pltpu.VMEM)
+    dma = pltpu.SemaphoreType.DMA
+    flat = jax.ShapeDtypeStruct((tok_count, features), low)
+    return pl.pallas_call(
+        functools.partial(backward_kernel, count, groups),
+        out_shape=(
+            jax.ShapeDtypeStruct((tok_count, block), low),
+            flat,
+            jax.ShapeDtypeStruct((tok_count, width), low),
+            flat,
+            flat,
+            flat,
+            jax.ShapeDtypeStruct((1, features), f32),
+        ),
+        in_specs=[vmem, vmem, pl.BlockSpec(memory_space=pl.ANY)] + [vmem] * 6,
+        out_specs=[vmem] * 7,
+        scratch_shapes=[
+            pltpu.VMEM((width, features), low),
+            pltpu.VMEM((groups, tok_count, block), low),
+            pltpu.VMEM((groups, tok_count, block), low),
+            pltpu.VMEM((tok_count, block), f32),
+            pltpu.VMEM((tok_count, 128), f32),
+            pltpu.VMEM((groups, tok_count, 128), f32),
+            pltpu.VMEM((tok_count, 128), f32),
+            pltpu.VMEM((groups, tok_count, 128), f32),
+            pltpu.VMEM((tok_count, features), f32),
+            pltpu.VMEM((tok_count, features), f32),
+            pltpu.VMEM((tok_count, features), low),
+            pltpu.VMEM(state.shape, low),
+            pltpu.VMEM(state.shape, low),
+            pltpu.VMEM(state.shape, low),
+            pltpu.VMEM(state.shape, low),
+            dma((groups,)),
+            dma((4, groups)),
+            dma((4, groups)),
+            dma((count,)),
+            dma((count,)),
+            dma((count,)),
+            dma((count,)),
+        ],
+        compiler_params=pltpu.CompilerParams(collective_id=1, has_side_effects=True),
+        name="backward_part",
+    )(mixed, gain, weight, target, queries, key_input, value_input, scores, state)
+
+
 def per_device(queries, key_input, value_input, norm_gain, out_weight, target):
-    tok_count = queries.shape[0]
-    local_heads = queries.shape[1] // HEAD_DIM
-    shape3 = (tok_count, local_heads, HEAD_DIM)
-    q_heads = queries.reshape(shape3)
-    k_heads = key_input.reshape(shape3)
-    v_heads = value_input.reshape(shape3)
-    keep_mask = causal(tok_count)
-    f32 = jnp.float32
-    gathered, mixed, scores_low, state_low = forward_part(
-        queries, key_input, value_input, out_weight.T
+    gathered, mixed, scores, state = forward_part(queries, key_input, value_input, out_weight.T)
+    full_weight = gathered.reshape(-1, gathered.shape[2])
+    output, normed, out_grad, query_grad, key_grad, value_grad, gain_grads = backward_part(
+        mixed,
+        norm_gain[None],
+        full_weight,
+        target,
+        queries,
+        key_input,
+        value_input,
+        scores,
+        state,
     )
-    state_low = state_low.reshape(local_heads, HEAD_DIM, HEAD_DIM)
-    full_weight = gathered.reshape(-1, gathered.shape[2])
-    gain_float = norm_gain.astype(f32)
-    squares = lax.psum(jnp.sum(mixed * mixed, axis=1, keepdims=True), "head")
-    inverse = lax.rsqrt(squares / FEATURES + EPSILON)
-    normed = (mixed * inverse * gain_float).astype(jnp.bfloat16)
-    partial_value = lax.dot_general(
-        normed, full_weight, (((1,), (1,)), ((), ())), preferred_element_type=f32
-    )
-    projected = lax.psum_scatter(
-        partial_value.astype(jnp.bfloat16), "head", scatter_dimension=1, tiled=True
-    ).astype(jnp.float32)
-    output = projected.astype(jnp.bfloat16)
-    grad_local = (projected - target.astype(f32)).astype(jnp.bfloat16)
-    out_grad = lax.all_gather(grad_local, "head", axis=1, tiled=True)
-    normed_grad = lax.dot_general(
-        out_grad, full_weight, (((1,), (0,)), ((), ())), preferred_element_type=f32
-    )
-    product = jnp.sum(grad_local.astype(f32) * projected, axis=1, keepdims=True)
-    inner = lax.psum(product, "head") / inverse
-    mixed_grad = inverse * gain_float * normed_grad - mixed * inverse**3 * inner / FEATURES
-    mixed_grad = mixed_grad.astype(jnp.bfloat16)
-    gain_grads = jnp.sum(normed_grad * mixed * inverse, axis=0)[None]
     weight_grads = lax.dot_general(
-        normed, out_grad, (((0,), (0,)), ((), ())), preferred_element_type=f32
+        normed, out_grad, (((0,), (0,)), ((), ())), preferred_element_type=jnp.float32
     ).astype(jnp.bfloat16)[None]
-    grad_heads = mixed_grad.reshape(shape3)
-    grad_state = jnp.einsum("thd,the->hde", q_heads, grad_heads, preferred_element_type=f32)
-    later_low = entering(grad_state, "seq", True)
-    pairs = jnp.einsum("thd,shd->hts", grad_heads, v_heads, preferred_element_type=f32)
-    pairs_low = jnp.where(keep_mask[None], pairs, 0.0).astype(jnp.bfloat16)
-    query_grad = jnp.einsum("hts,shd->thd", pairs_low, k_heads, preferred_element_type=f32)
-    query_grad = query_grad + jnp.einsum(
-        "the,hde->thd", grad_heads, state_low, preferred_element_type=f32
-    )
-    key_grad = jnp.einsum("hts,thd->shd", pairs_low, q_heads, preferred_element_type=f32)
-    key_grad = key_grad + jnp.einsum("she,hde->shd", v_heads, later_low, preferred_element_type=f32)
-    value_grad = jnp.einsum("hts,the->she", scores_low, grad_heads, preferred_element_type=f32)
-    value_grad = value_grad + jnp.einsum(
-        "shd,hde->she", k_heads, later_low, preferred_element_type=f32
-    )
-    flat_shape = (tok_count, -1)
-    return (
-        output,
-        query_grad.reshape(flat_shape).astype(jnp.bfloat16),
-        key_grad.reshape(flat_shape).astype(jnp.bfloat16),
-        value_grad.reshape(flat_shape).astype(jnp.bfloat16),
-        gain_grads,
-        weight_grads,
-    )
+    return output, query_grad, key_grad, value_grad, gain_grads, weight_grads
 
 
 def solution(mesh):

time: 255 us -> 204 us (0.80)
  Pallas kernels: 132 us -> 185 us
  matrix products: 51.7 us -> 10.1 us
  waiting for transfers between devices: 24.6 us -> 0 us
  between operations: 14.2 us -> 0.67 us
  starting transfers between devices: 11.2 us -> 0 us
  local copies, waits for them, and re-layouts: 11.2 us -> 5.7 us
  blocking collectives: 4.94 us -> 0 us
  other arithmetic: 4.3 us -> 0 us
    pallas_call x0 -> x1, Pallas kernels: none -> 52.8 us  [backward_part(): pl.pallas_call(functools.partial(backward_kernel, count, groups), out_sha...]
    dot_general x11 -> x0, matrix products: 45 us -> none  [the longest x1 14.1 us: per_device(): lax.dot_general(normed, full_weight, (((1,), (1,)), ((), ())), preferred_...]
    all_to_all x2 -> x0, starting transfers between devices: 11.1 us -> none  [the longest x1 6.86 us: entering(): spread = lax.all_to_all(pieces, axis, 0, 0)]
    all_gather x1 -> x0, waiting for transfers between devices: 8.71 us -> none  [per_device(): out_grad = lax.all_gather(grad_local, 'head', axis=1, tiled=True)]
    all_to_all x2 -> x0, waiting for transfers between devices: 8.68 us -> none  [the longest x1 4.52 us: entering(): spread = lax.all_to_all(pieces, axis, 0, 0)]
    reduce_scatter x1 -> x0, waiting for transfers between devices: 7.15 us -> none  [per_device(): lax.psum_scatter(partial_value.astype(jnp.bfloat16), 'head', scatter_dime...]
    psum x2 -> x0, blocking collectives: 4.94 us -> none  [the longest x1 2.47 us: per_device(): inner = lax.psum(product, 'head') / inverse]
    reduce_sum x2 -> x0, other arithmetic: 4.25 us -> none  [the longest x1 2.29 us: per_device(): product = jnp.sum(grad_local.astype(f32) * projected, axis=1, keepdims=True)]
  transfers between devices with their start and end apart: 4 -> 0, of which waited for: 4 -> 0; matrix products, arithmetic and copies ran while one was open for 8% -> 0% of each run, Pallas kernels for 0% -> 0%
where the time goes in v3:
time: 204 us; the launch traced here: 201 us
  Pallas kernels  185 us (91%)
  matrix products  10.1 us (5%)
  local copies, waits for them, and re-layouts  5.7 us (3%)
    pallas_call x1, Pallas kernels, forward_part(): pl.pallas_call(functools.partial(forward_kernel, count), out_shape=(jax.S...  132 us
    pallas_call x1, Pallas kernels, backward_part(): pl.pallas_call(functools.partial(backward_kernel, count, groups), out_sha...  52.8 us
    dot_general x1, matrix products, per_device(): lax.dot_general(normed, out_grad, (((0,), (0,)), ((), ())), preferred_ele...  10.1 us
    unnamed x15, local copies, waits for them, and re-layouts  4.41 us

profile of v3, /device:TPU:0, one launch (start us, length us, event | category | flops | bytes accessed | tf_op | source)
XLA Modules:
  0.0 201.4 jit_solution(8914048993826794182)
XLA Ops:
  0.6 1.3 broadcast_in_dim.6.gain_ref
  1.9 132.1 %forward_part.1 = (bf16[16,192,2048]{2,1,0:T(8,128)(2,1)}, f32[256,2048]{1,0:T(8,128)}, bf16[16,256,256]{2,1,0:T(8,128)(2,1)}, bf16[16,128,128]{2,1,0:T(8,128)(2,1)}) custom-call(bf16[256,2048]{1,0:T(8,128)(2,1)} %q_ref.3, bf16[256,2048]{1,0:T(8,128)(2,1)} %k_ref.3, bf16[256,2048]{1,0:T(8,128)(2,1)} %v_ref.3, bf16[192,2048]{1,0:T(8,128)(2,1)} %bitcast.7), custom_call_target="tpu_custom_call" | custom-call | tf_op jit(solution)/shard_map/forward_part/pallas_call | solution.py:316
  134.0 52.8 %backward_part.1 = (bf16[256,1536]{1,0:T(8,128)(2,1)}, bf16[256,2048]{1,0:T(8,128)(2,1)}, bf16[256,3072]{1,0:T(8,128)(2,1)}, bf16[256,2048]{1,0:T(8,128)(2,1)}, ...) custom-call(f32[256,2048]{1,0:T(8,128)} %get-tuple-element.17.mixed_ref, ...), custom_call_target="tpu_custom_call" | custom-call | tf_op jit(solution)/shard_map/backward_part/pallas_call | solution.py:586
  186.9 0.0 copy-start.3
  186.9 0.0 copy-start.2
  186.9 10.1 %convert_bitcast_fusion = bf16[1,2048,3072]{2,1,0:T(8,128)(2,1)} fusion(bf16[256,2048]{1,0:T(8,128)(2,1)} %get-tuple-element.26, bf16[256,3072]{1,0:T(8,128)(2,1)} %get-tuple-element.27), kind=kOutput, calls=%fused_computation | convolution fusion | flops 3227516928 | bytes 15204352 | tf_op jit(solution)/shard_map/dot_general | solution.py:642
  197.0 0.0 copy-done.3
  197.0 0.0 copy-start.1
  197.0 0.9 copy.17
  197.9 0.0 copy-done.2
  197.9 0.0 copy-start
  197.9 1.0 copy.18
  198.8 0.0 copy-done.1
  198.8 0.0 copy-start.4
  198.8 1.0 copy.19
  199.8 0.0 copy-done
  199.8 1.0 copy.20
  200.8 0.0 copy-done.4
  200.8 0.6 copy.21
Async XLA Ops:
  186.9 10.1 %copy-start.3 = (bf16[256,1536]{1,0:T(8,128)(2,1)S(1)}, bf16[256,1536]{1,0:T(8,128)(2,1)}, u32[]{:S(2)}) copy-start(bf16[256,1536]{1,0:T(8,128)(2,1)} %get-tuple-element.34) | copy-start | bytes 2359300
  186.9 11.0 %copy-start.2 = (bf16[256,2048]{1,0:T(8,128)(2,1)S(1)}, bf16[256,2048]{1,0:T(8,128)(2,1)}, u32[]{:S(2)}) copy-start(bf16[256,2048]{1,0:T(8,128)(2,1)} %get-tuple-element.35) | copy-start | bytes 3145732
  197.0 1.9 copy-start.1
  197.9 1.9 copy-start
  198.8 1.9 copy-start.4

commit v4 on v3

--- a/solution.py
+++ b/solution.py
@@ -125,7 +125,7 @@
     y_peer = layer * 4 + plane_y
     features = w_ref.shape[1]
     blocks = features // 128
-    cut_a = blocks // 4
+    cut_a = max(1, blocks * 3 // 16)
     cut_b = cut_a + (blocks - cut_a + 1) // 2
     edges = (0, cut_a * 128, cut_b * 128, features)
     piece = [pl.ds(edges[i], edges[i + 1] - edges[i]) for i in range(3)]
@@ -240,10 +240,6 @@
                 vertical(up, at, 2 + slot, shard, 0, act, slack=slack)
 
     greet(("seq", count, me))
-    own_sends(begin)
-    own = pltpu.make_async_copy(w_ref, full_ref.at[me], own_sem)
-    own.start()
-
     def outer(head, carry):
         cols = columns_of(head)
         state = lax.dot_general(
@@ -255,6 +251,10 @@
 
     lax.fori_loop(0, local_heads, outer, 0)
     exchange(count, me, mine_ref, spread_ref, first_send, first_recv)
+    own_sends(begin)
+    own = pltpu.make_async_copy(w_ref, full_ref.at[me], own_sem)
+    own.start()
+
     keep = causal(tok_count)
 
     def inside(head, carry):
@@ -268,16 +268,18 @@
         return carry
 
     lax.fori_loop(0, local_heads, inside, 0)
+    exchange_wait(count, me, mine_ref, spread_ref, first_send, first_recv)
+    running_sums(count, spread_ref, sums_ref, False)
+    exchange(count, me, sums_ref, state_ref, second_send, second_recv)
     column_step(1, begin, True)
     diagonal_step(0, begin, True)
     plane_step(begin, True)
-    exchange_wait(count, me, mine_ref, spread_ref, first_send, first_recv)
-    running_sums(count, spread_ref, sums_ref, False)
-    exchange(count, me, sums_ref, state_ref, second_send, second_recv)
     for step in range(2, layers):
         column_step(step, begin, True)
         diagonal_step(step - 1, begin, True)
         plane_chain(step - 1, begin, True)
+    diagonal_step(layers - 1, begin, True)
+    plane_chain(layers - 1, begin, True)
     exchange_wait(count, me, sums_ref, state_ref, second_send, second_recv)
 
     def across(head, carry):
@@ -287,8 +289,6 @@
         return carry
 
     lax.fori_loop(0, local_heads, across, 0)
-    diagonal_step(layers - 1, begin, True)
-    plane_chain(layers - 1, begin, True)
     for at in range(layers):
         landed(at * 4 + plane_x, 1)
         landed(at * 4 + plane_y, 2)

time: 204 us -> 200 us (0.980)
  Pallas kernels: 185 us -> 181 us
    pallas_call x1, Pallas kernels: 132 us -> 129 us  [forward_part(): pl.pallas_call(functools.partial(forward_kernel, count), out_shape=(jax.S...]
where the time goes in v4:
time: 200 us; the launch traced here: 198 us
  Pallas kernels  181 us (90%)
  matrix products  10.1 us (5%)
  local copies, waits for them, and re-layouts  5.7 us (3%)
    pallas_call x1, Pallas kernels, forward_part(): pl.pallas_call(functools.partial(forward_kernel, count), out_shape=(jax.S...  129 us
    pallas_call x1, Pallas kernels, backward_part(): pl.pallas_call(functools.partial(backward_kernel, count, groups), out_sha...  52.6 us
    dot_general x1, matrix products, per_device(): lax.dot_general(normed, out_grad, (((0,), (0,)), ((), ())), preferred_ele...  10.1 us
    unnamed x15, local copies, waits for them, and re-layouts  4.41 us

profile of v4, /device:TPU:0, one launch (start us, length us, event | category | flops | bytes accessed | tf_op | source)
XLA Modules:
  0.0 197.9 jit_solution(14706633694593743032)
XLA Ops:
  0.6 1.3 broadcast_in_dim.6.gain_ref
  1.9 128.8 %forward_part.1 = (bf16[16,192,2048]{2,1,0:T(8,128)(2,1)}, f32[256,2048]{1,0:T(8,128)}, bf16[16,256,256]{2,1,0:T(8,128)(2,1)}, bf16[16,128,128]{2,1,0:T(8,128)(2,1)}) custom-call(bf16[256,2048]{1,0:T(8,128)(2,1)} %q_ref.3, bf16[256,2048]{1,0:T(8,128)(2,1)} %k_ref.3, bf16[256,2048]{1,0:T(8,128)(2,1)} %v_ref.3, bf16[192,2048]{1,0:T(8,128)(2,1)} %bitcast.7), custom_call_target="tpu_custom_call" | custom-call | tf_op jit(solution)/shard_map/forward_part/pallas_call | solution.py:316
  130.8 52.6 %backward_part.1 = (bf16[256,1536]{1,0:T(8,128)(2,1)}, bf16[256,2048]{1,0:T(8,128)(2,1)}, bf16[256,3072]{1,0:T(8,128)(2,1)}, bf16[256,2048]{1,0:T(8,128)(2,1)}, ...) custom-call(f32[256,2048]{1,0:T(8,128)} %get-tuple-element.17.mixed_ref, ...), custom_call_target="tpu_custom_call" | custom-call | tf_op jit(solution)/shard_map/backward_part/pallas_call | solution.py:586
  183.3 0.0 copy-start.3
  183.3 0.0 copy-start.2
  183.4 10.1 %convert_bitcast_fusion = bf16[1,2048,3072]{2,1,0:T(8,128)(2,1)} fusion(bf16[256,2048]{1,0:T(8,128)(2,1)} %get-tuple-element.26, bf16[256,3072]{1,0:T(8,128)(2,1)} %get-tuple-element.27), kind=kOutput, calls=%fused_computation | convolution fusion | flops 3227516928 | bytes 15204352 | tf_op jit(solution)/shard_map/dot_general | solution.py:642
  193.5 0.0 copy-done.3
  193.5 0.0 copy-start.1
  193.5 0.9 copy.17
  194.3 0.0 copy-done.2
  194.3 0.0 copy-start
  194.4 1.0 copy.18
  195.3 0.0 copy-done.1
  195.3 0.0 copy-start.4
  195.3 1.0 copy.19
  196.3 0.0 copy-done
  196.3 1.0 copy.20
  197.3 0.0 copy-done.4
  197.3 0.6 copy.21
Async XLA Ops:
  183.3 10.1 %copy-start.3 = (bf16[256,1536]{1,0:T(8,128)(2,1)S(1)}, bf16[256,1536]{1,0:T(8,128)(2,1)}, u32[]{:S(2)}) copy-start(bf16[256,1536]{1,0:T(8,128)(2,1)} %get-tuple-element.34) | copy-start | bytes 2359300
  183.3 11.0 %copy-start.2 = (bf16[256,2048]{1,0:T(8,128)(2,1)S(1)}, bf16[256,2048]{1,0:T(8,128)(2,1)}, u32[]{:S(2)}) copy-start(bf16[256,2048]{1,0:T(8,128)(2,1)} %get-tuple-element.35) | copy-start | bytes 3145732
  193.5 1.9 copy-start.1
  194.3 1.9 copy-start
  195.3 1.9 copy-start.4

commit v5 on v4

--- a/solution.py
+++ b/solution.py
@@ -89,12 +89,22 @@
     return (((left,), (right,)), ((), ()))
 
 
-def forward_kernel(
+def kernel(
     count,
+    groups,
     q_ref,
     k_ref,
     v_ref,
     w_ref,
+    gain_ref,
+    target_ref,
+    output_ref,
+    normed_ref,
+    out_grad_ref,
+    query_ref,
+    key_ref,
+    value_ref,
+    gain_grad_ref,
     full_ref,
     mixed_ref,
     scores_ref,
@@ -102,19 +112,41 @@
     mine_ref,
     spread_ref,
     sums_ref,
+    later_mine_ref,
+    later_spread_ref,
+    later_sums_ref,
+    later_ref,
+    part_mine,
+    part_land,
+    own_part,
+    square_mine,
+    square_land,
+    product_mine,
+    product_land,
+    normed_grad_ref,
+    key_part,
+    mixed_grad_ref,
     x_sem,
     y_sem,
     up_sem,
     down_sem,
     land_sem,
+    own_sem,
+    head_send,
+    head_recv,
     first_send,
     first_recv,
     second_send,
     second_recv,
-    own_sem,
+    back_first_send,
+    back_first_recv,
+    back_second_send,
+    back_second_recv,
 ):
     f32 = jnp.float32
+    low = jnp.bfloat16
     me = lax.axis_index("seq")
+    group = lax.axis_index("head")
     layers = count // 4
     layer, plane = me // 4, lax.rem(me, 4)
     row, col = plane // 2, lax.rem(plane, 2)
@@ -133,11 +165,15 @@
     per_head = HEAD_DIM // mine_ref.shape[1]
     tok_count = q_ref.shape[0]
 
+    share = w_ref.shape[0]
+
+    def shard_rows(shard):
+        return pl.ds(pl.multiple_of(shard * share, share), share)
+
     def copy(shard, part, send_sem, peer, own=False):
-        src = w_ref.at[:, piece[part]] if own else full_ref.at[shard, :, piece[part]]
-        return remote(
-            src, full_ref.at[shard, :, piece[part]], send_sem, land_sem.at[shard, part], peer
-        )
+        target = full_ref.at[shard_rows(shard), piece[part]]
+        src = w_ref.at[:, piece[part]] if own else target
+        return remote(src, target, send_sem, land_sem.at[shard, part], peer)
 
     def landed(shard, part):
         copy(shard, part, x_sem.at[layers, 2], x_peer).wait_recv()
@@ -239,7 +275,7 @@
 
                 vertical(up, at, 2 + slot, shard, 0, act, slack=slack)
 
-    greet(("seq", count, me))
+    greet(("seq", count, me), ("head", groups, group))
     def outer(head, carry):
         cols = columns_of(head)
         state = lax.dot_general(
@@ -252,7 +288,7 @@
     lax.fori_loop(0, local_heads, outer, 0)
     exchange(count, me, mine_ref, spread_ref, first_send, first_recv)
     own_sends(begin)
-    own = pltpu.make_async_copy(w_ref, full_ref.at[me], own_sem)
+    own = pltpu.make_async_copy(w_ref, full_ref.at[shard_rows(me)], own_sem)
     own.start()
 
     keep = causal(tok_count)
@@ -289,112 +325,9 @@
         return carry
 
     lax.fori_loop(0, local_heads, across, 0)
-    for at in range(layers):
-        landed(at * 4 + plane_x, 1)
-        landed(at * 4 + plane_y, 2)
-        landed(at * 4 + plane_d, 1)
-        landed(at * 4 + plane_d, 2)
-    own_sends(finish)
-    plane_step(finish, False)
-    diagonal_step(0, finish, False)
-    for step in range(1, layers):
-        column_step(step, finish, False)
-        diagonal_step(step, finish, False)
-        plane_chain(step, finish, False)
-    own.wait()
-
-
-def forward_part(queries, key_input, value_input, weight):
-    count = lax.axis_size("seq")
-    tok_count, features = queries.shape
-    local_heads = features // HEAD_DIM
-    layers = count // 4
-    piece_shape = (count, local_heads * HEAD_DIM // count, HEAD_DIM)
-    low = jnp.bfloat16
-    vmem = pl.BlockSpec(memory_space=pltpu.VMEM)
-    dma = pltpu.SemaphoreType.DMA
-    return pl.pallas_call(
-        functools.partial(forward_kernel, count),
-        out_shape=(
-            jax.ShapeDtypeStruct((count,) + weight.shape, low),
-            jax.ShapeDtypeStruct((tok_count, features), jnp.float32),
-            jax.ShapeDtypeStruct((local_heads, tok_count, tok_count), low),
-            jax.ShapeDtypeStruct(piece_shape, low),
-        ),
-        in_specs=[vmem] * 4,
-        out_specs=(pl.BlockSpec(memory_space=pl.ANY), vmem, vmem, vmem),
-        scratch_shapes=[
-            pltpu.VMEM(piece_shape, low),
-            pltpu.VMEM(piece_shape, low),
-            pltpu.VMEM(piece_shape, low),
-            dma((layers + 1, 3)),
-            dma((layers + 1, 3)),
-            dma((layers, 6)),
-            dma((layers, 6)),
-            dma((count, 3)),
-            dma((count,)),
-            dma((count,)),
-            dma((count,)),
-            dma((count,)),
-            dma(()),
-        ],
-        compiler_params=pltpu.CompilerParams(collective_id=0, has_side_effects=True),
-        name="forward_part",
-    )(queries, key_input, value_input, weight)
-
-
-def backward_kernel(
-    count,
-    groups,
-    mixed_ref,
-    gain_ref,
-    w_hbm,
-    target_ref,
-    q_ref,
-    k_ref,
-    v_ref,
-    scores_ref,
-    state_ref,
-    output_ref,
-    normed_ref,
-    out_grad_ref,
-    query_ref,
-    key_ref,
-    value_ref,
-    gain_grad_ref,
-    w_ref,
-    part_mine,
-    part_land,
-    own_part,
-    square_mine,
-    square_land,
-    product_mine,
-    product_land,
-    normed_grad_ref,
-    key_part,
-    mixed_grad_ref,
-    mine_ref,
-    spread_ref,
-    sums_ref,
-    later_ref,
-    w_sem,
-    head_send,
-    head_recv,
-    first_send,
-    first_recv,
-    second_send,
-    second_recv,
-):
-    f32 = jnp.float32
-    low = jnp.bfloat16
-    me = lax.axis_index("seq")
-    group = lax.axis_index("head")
-    tok_count, features = q_ref.shape
     block = target_ref.shape[1]
     tile = 256 if block % 256 == 0 else 128
     wide = 256
-    local_heads = features // HEAD_DIM
-    per_head = HEAD_DIM // mine_ref.shape[1]
     ahead = [lax.rem(group + step, groups) for step in range(groups)]
     behind = [lax.rem(group + groups - step, groups) for step in range(groups)]
 
@@ -403,10 +336,6 @@
 
     def tile_of(index, size, base=0):
         return pl.ds(pl.multiple_of(base + index * size, size), size)
-
-    def w_copy(step):
-        rows = block_rows(ahead[step])
-        return pltpu.make_async_copy(w_hbm.at[rows], w_ref.at[rows], w_sem.at[step])
 
     def head_copy(kind, step, src, dst):
         return remote(
@@ -427,9 +356,6 @@
         return head_copy(3, step, out_grad_ref.at[:, cols], out_grad_ref.at[:, cols])
 
     order = list(range(1, groups)) + [0]
-    for step in order:
-        w_copy(step).start()
-    greet(("seq", count, me), ("head", groups, group))
 
     def squared(index, total):
         value = mixed_ref[:, tile_of(index, wide)]
@@ -452,13 +378,18 @@
 
     lax.fori_loop(0, features // wide, normalize, 0)
 
+    for at in range(layers):
+        landed(at * 4 + plane_x, 1)
+        landed(at * 4 + plane_y, 2)
+        landed(at * 4 + plane_d, 1)
+        landed(at * 4 + plane_d, 2)
+    own.wait()
     for step in order:
-        w_copy(step).wait()
 
         def project(index, carry, step=step):
             rows = tile_of(index, tile, ahead[step] * block)
             value = lax.dot_general(
-                normed_ref[...], w_ref[rows, :], dims(1, 1), preferred_element_type=f32
+                normed_ref[...], full_ref[rows, :], dims(1, 1), preferred_element_type=f32
             )
             if step:
                 part_mine[step, :, tile_of(index, tile)] = value.astype(low)
@@ -472,7 +403,7 @@
     for step in range(1, groups):
         part_copy(step).wait()
 
-    def finish(index, total):
+    def settle(index, total):
         cols = tile_of(index, tile)
         projected = own_part[:, cols]
         for step in range(1, groups):
@@ -482,7 +413,7 @@
         out_grad_ref[:, tile_of(index, tile, group * block)] = grad
         return total + jnp.sum(grad.astype(f32) * projected, axis=1, keepdims=True)
 
-    product = lax.fori_loop(0, block // tile, finish, jnp.zeros((tok_count, 1), f32))
+    product = lax.fori_loop(0, block // tile, settle, jnp.zeros((tok_count, 1), f32))
     product_mine[...] = jnp.broadcast_to(product, product_mine.shape)
     for step in range(1, groups):
         grad_copy(step, group).start()
@@ -492,7 +423,7 @@
         cols = tile_of(index, wide)
         rows = block_rows(group)
         normed_grad_ref[:, cols] = jnp.dot(
-            out_grad_ref[:, rows], w_ref[rows, cols], preferred_element_type=f32
+            out_grad_ref[:, rows], full_ref[rows, cols], preferred_element_type=f32
         )
         return carry
 
@@ -511,7 +442,7 @@
         for step in range(1, groups):
             rows = block_rows(behind[step])
             grad = grad + jnp.dot(
-                out_grad_ref[:, rows], w_ref[rows, cols], preferred_element_type=f32
+                out_grad_ref[:, rows], full_ref[rows, cols], preferred_element_type=f32
             )
         mixed = mixed_ref[:, cols]
         gain = gain_ref[:, cols].astype(f32)
@@ -526,15 +457,14 @@
                 dims(0, 0),
                 preferred_element_type=f32,
             )
-            state = state.reshape((per_head,) + mine_ref.shape[1:])
-            mine_ref[pieces_of(head, per_head)] = state.astype(low)
+            state = state.reshape((per_head,) + later_mine_ref.shape[1:])
+            later_mine_ref[pieces_of(head, per_head)] = state.astype(low)
         return carry
 
     lax.fori_loop(0, features // wide, rest, 0)
-    exchange(count, me, mine_ref, spread_ref, first_send, first_recv)
-    keep = causal(tok_count)
-
-    def inside(head, carry):
+    exchange(count, me, later_mine_ref, later_spread_ref, back_first_send, back_first_recv)
+
+    def paired(head, carry):
         cols = columns_of(head)
         grad = mixed_grad_ref[:, cols]
         pairs = lax.dot_general(grad, v_ref[:, cols], dims(1, 1), preferred_element_type=f32)
@@ -555,12 +485,12 @@
         )
         return carry
 
-    lax.fori_loop(0, local_heads, inside, 0)
-    exchange_wait(count, me, mine_ref, spread_ref, first_send, first_recv)
-    running_sums(count, spread_ref, sums_ref, True)
-    exchange(count, me, sums_ref, later_ref, second_send, second_recv)
+    lax.fori_loop(0, local_heads, paired, 0)
+    exchange_wait(count, me, later_mine_ref, later_spread_ref, back_first_send, back_first_recv)
+    running_sums(count, later_spread_ref, later_sums_ref, True)
+    exchange(count, me, later_sums_ref, later_ref, back_second_send, back_second_recv)
     lax.fori_loop(0, local_heads, values, 0)
-    exchange_wait(count, me, sums_ref, later_ref, second_send, second_recv)
+    exchange_wait(count, me, later_sums_ref, later_ref, back_second_send, back_second_recv)
 
     def last(head, carry):
         cols = columns_of(head)
@@ -572,19 +502,29 @@
         return carry
 
     lax.fori_loop(0, local_heads, last, 0)
-
-
-def backward_part(mixed, gain, weight, target, queries, key_input, value_input, scores, state):
+    own_sends(finish)
+    plane_step(finish, False)
+    diagonal_step(0, finish, False)
+    for step in range(1, layers):
+        column_step(step, finish, False)
+        diagonal_step(step, finish, False)
+        plane_chain(step, finish, False)
+
+
+def fused(queries, key_input, value_input, weight, gain, target):
     count, groups = lax.axis_size("seq"), lax.axis_size("head")
     tok_count, features = queries.shape
+    local_heads = features // HEAD_DIM
+    layers = count // 4
     block = target.shape[1]
-    width = weight.shape[0]
+    width = count * weight.shape[0]
     low, f32 = jnp.bfloat16, jnp.float32
+    pieces = pltpu.VMEM((count, local_heads * HEAD_DIM // count, HEAD_DIM), low)
+    flat = jax.ShapeDtypeStruct((tok_count, features), low)
     vmem = pl.BlockSpec(memory_space=pltpu.VMEM)
     dma = pltpu.SemaphoreType.DMA
-    flat = jax.ShapeDtypeStruct((tok_count, features), low)
     return pl.pallas_call(
-        functools.partial(backward_kernel, count, groups),
+        functools.partial(kernel, count, groups),
         out_shape=(
             jax.ShapeDtypeStruct((tok_count, block), low),
             flat,
@@ -594,10 +534,15 @@
             flat,
             jax.ShapeDtypeStruct((1, features), f32),
         ),
-        in_specs=[vmem, vmem, pl.BlockSpec(memory_space=pl.ANY)] + [vmem] * 6,
+        in_specs=[vmem] * 6,
         out_specs=[vmem] * 7,
         scratch_shapes=[
             pltpu.VMEM((width, features), low),
+            pltpu.VMEM((tok_count, features), f32),
+            pltpu.VMEM((local_heads, tok_count, tok_count), low),
+        ]
+        + [pieces] * 8
+        + [
             pltpu.VMEM((groups, tok_count, block), low),
             pltpu.VMEM((groups, tok_count, block), low),
             pltpu.VMEM((tok_count, block), f32),
@@ -608,36 +553,24 @@
             pltpu.VMEM((tok_count, features), f32),
             pltpu.VMEM((tok_count, features), f32),
             pltpu.VMEM((tok_count, features), low),
-            pltpu.VMEM(state.shape, low),
-            pltpu.VMEM(state.shape, low),
-            pltpu.VMEM(state.shape, low),
-            pltpu.VMEM(state.shape, low),
-            dma((groups,)),
+            dma((layers + 1, 3)),
+            dma((layers + 1, 3)),
+            dma((layers, 6)),
+            dma((layers, 6)),
+            dma((count, 3)),
+            dma(()),
             dma((4, groups)),
             dma((4, groups)),
-            dma((count,)),
-            dma((count,)),
-            dma((count,)),
-            dma((count,)),
-        ],
-        compiler_params=pltpu.CompilerParams(collective_id=1, has_side_effects=True),
-        name="backward_part",
-    )(mixed, gain, weight, target, queries, key_input, value_input, scores, state)
+        ]
+        + [dma((count,))] * 8,
+        compiler_params=pltpu.CompilerParams(collective_id=0, has_side_effects=True),
+        name="fused",
+    )(queries, key_input, value_input, weight, gain, target)
 
 
 def per_device(queries, key_input, value_input, norm_gain, out_weight, target):
-    gathered, mixed, scores, state = forward_part(queries, key_input, value_input, out_weight.T)
-    full_weight = gathered.reshape(-1, gathered.shape[2])
-    output, normed, out_grad, query_grad, key_grad, value_grad, gain_grads = backward_part(
-        mixed,
-        norm_gain[None],
-        full_weight,
-        target,
-        queries,
-        key_input,
-        value_input,
-        scores,
-        state,
+    output, normed, out_grad, query_grad, key_grad, value_grad, gain_grads = fused(
+        queries, key_input, value_input, out_weight.T, norm_gain[None], target
     )
     weight_grads = lax.dot_general(
         normed, out_grad, (((0,), (0,)), ((), ())), preferred_element_type=jnp.float32

time: 200 us -> 190 us (0.950)
  Pallas kernels: 181 us -> 169 us
    pallas_call x2 -> x1, Pallas kernels: 181 us -> 169 us  [fused(): pl.pallas_call(functools.partial(kernel, count, groups), out_shape=(jax.S...]
where the time goes in v5:
time: 190 us; the launch traced here: 187 us
  Pallas kernels  169 us (89%)
  matrix products  10.1 us (5%)
  local copies, waits for them, and re-layouts  6.33 us (3%)
    pallas_call x1, Pallas kernels, fused(): pl.pallas_call(functools.partial(kernel, count, groups), out_shape=(jax.S...  169 us
    dot_general x1, matrix products, per_device(): lax.dot_general(normed, out_grad, (((0,), (0,)), ((), ())), preferred_ele...  10.1 us
    unnamed x15, local copies, waits for them, and re-layouts  5.04 us

profile of v5, /device:TPU:0, one launch (start us, length us, event | category | flops | bytes accessed | tf_op | source)
XLA Modules:
  0.0 186.5 jit_solution(18003499211374471710)
XLA Ops:
  0.6 1.3 broadcast_in_dim.6.gain_ref
  1.9 169.4 %fused.1 = (bf16[256,1536]{1,0:T(8,128)(2,1)}, bf16[256,2048]{1,0:T(8,128)(2,1)}, bf16[256,3072]{1,0:T(8,128)(2,1)}, bf16[256,2048]{1,0:T(8,128)(2,1)}, bf16[256...) custom-call(bf16[256,2048]{1,0:T(8,128)(2,1)} %q_ref.1, bf16[256,2048]{1,0:T(8,128)(2,1)} %k_ref.1, ...), custom_call_target="tpu_custom_call" | custom-call | tf_op jit(solution)/shard_map/fused/pallas_call | solution.py:526
  171.3 0.0 copy-start.3
  171.4 0.0 copy-start.2
  171.4 10.1 %convert_bitcast_fusion = bf16[1,2048,3072]{2,1,0:T(8,128)(2,1)} fusion(bf16[256,2048]{1,0:T(8,128)(2,1)} %get-tuple-element.18, bf16[256,3072]{1,0:T(8,128)(2,1)} %get-tuple-element.19), kind=kOutput, calls=%fused_computation | convolution fusion | flops 3227516928 | bytes 15204352 | tf_op jit(solution)/shard_map/dot_general | solution.py:575
  181.5 0.0 copy-done.3
  181.5 0.0 copy-start.1
  181.5 0.9 copy.17
  182.4 0.0 copy-done.2
  182.4 1.0 copy.18
  183.3 0.0 copy-done.1
  183.3 0.0 copy-start
  183.3 1.0 copy.19
  184.3 0.6 copy-done
  184.9 0.0 copy-start.4
  184.9 1.0 copy.20
  185.9 0.0 copy-done.4
  185.9 0.6 copy.21
Async XLA Ops:
  171.3 10.1 %copy-start.3 = (bf16[256,1536]{1,0:T(8,128)(2,1)S(1)}, bf16[256,1536]{1,0:T(8,128)(2,1)}, u32[]{:S(2)}) copy-start(bf16[256,1536]{1,0:T(8,128)(2,1)} %get-tuple-element.26) | copy-start | bytes 2359300
  171.4 11.0 %copy-start.2 = (bf16[256,2048]{1,0:T(8,128)(2,1)S(1)}, bf16[256,2048]{1,0:T(8,128)(2,1)}, u32[]{:S(2)}) copy-start(bf16[256,2048]{1,0:T(8,128)(2,1)} %get-tuple-element.27) | copy-start | bytes 3145732
  181.5 1.9 copy-start.1
  183.3 1.6 copy-start
  184.9 1.0 copy-start.4
